TPU v7x, 128 devices: a whole 4x4x4 slice. The times are simulated.
128 devices in a mesh: tm: 4 (over x), det: 32 (over z, y, core).
Axes of the slice: x: 4, y: 4, z: 4, core: 2. Of those that a mesh axis runs over, the one named last changes fastest.
Arguments:
- timestream: float32 [4, 512, 8192], P('tm', 'det'), may hold values from -0.8 to 0.8
- polar_angle: float32 [4, 512, 8192], P('tm', 'det'), may hold values from -3.140625 to 3.140625
- pixel_index: int32 [4, 512, 8192], P('tm', 'det'), may hold values from 0 to 2047
- strip_tile: int32 [4, 512, 64], P('tm', 'det'), may hold values from 0 to 31
- time_const: float32 [4, 512], P('tm', 'det'), may hold values from 0.2 to 2
- knee_freq: float32 [4, 512], P('tm', 'det'), may hold values from 0.005 to 0.05
- noise_slope: float32 [4, 512], P('tm', 'det'), may hold values from 1 to 3
- white_weight: float32 [4, 512], P('tm', 'det'), may hold values from 0.5 to 2
- mode_mix: float32 [4, 512, 64], P('tm', 'det'), may hold values from -0.5 to 0.5
- coupling: float32 [64, 64], replicated, may hold values from -1 to 2
- device_slots: int32 [4, 1024], P('tm', 'det'), may hold values from 0 to 127, as said below
- slot_home: int32 [4, 128], P('tm', 'det'), may hold values from 0 to 31, as said below
Outputs:
- sky_map: float32 [1024, 3, 2048], P(('tm', 'det'))
Inputs may be any that keep to these rules, and one draw needn't show every extreme that they name: `device_slots`: entries j * 32 to (j + 1) * 32 - 1 of a row are the entries of the group's tile list that device j of the group touches, all distinct. Of each block of 4 entries (those with the same entry // 4) a device touches exactly 2 in half of the blocks and exactly 0 in the others. `slot_home`: entry s of group g is owner_tm * 8 + place: the tile is held at place place by the device with tm index owner_tm and det index s // 4. Entries of one block of 4 are distinct; in every block exactly 2 entries share one owner_tm, and the others are spread as evenly as possible over the other owner_tm values.
All inputs are finite; a program needn't handle non-finite values.
Results may differ from a plain program's by a relative error of at most 0.0001.
Values sent between devices are 32-bit elements; how exact they have to be, the bound alone decides.
No kernel may reach another device: no remote copies, remote signals or barrier semaphores. Data moves between devices by JAX's collectives and lax.ppermute only.
A program may use at most 64 MiB of HBM per device.

v0:
```python
import math

import jax
import jax.numpy as jnp
from jax import lax
from jax.sharding import PartitionSpec as P

SAMPLES = 4096
TILE_PIX = 2048
CAPT = 2
OWN = 8


HIGHEST = lax.Precision.HIGHEST


def fourier_table(length):
    counter = jnp.arange(length, dtype=jnp.int32)
    phases = counter[:, None] * counter[None, :] % length
    radians = 2.0 * math.pi / length * phases.astype(jnp.float32)
    return (jnp.cos(radians), jnp.sin(radians))


def twiddle_table(outer, inner, length):
    phases = (
        jnp.arange(outer, dtype=jnp.int32)[:, None]
        * jnp.arange(inner, dtype=jnp.int32)[None, :]
        % length
    )
    radians = 2.0 * math.pi / length * phases.astype(jnp.float32)
    return (jnp.cos(radians), jnp.sin(radians))


def forward_transform(signal):
    count, length = signal.shape
    outer = length // 128
    cos_outer, sin_outer = fourier_table(outer)
    cos_inner, sin_inner = fourier_table(128)
    cos_twist, sin_twist = twiddle_table(outer, 128, length)
    shaped = signal.reshape(count, outer, 128)
    first_real = jnp.einsum("rab,ak->rkb", shaped, cos_outer, precision=HIGHEST)
    first_imag = -jnp.einsum("rab,ak->rkb", shaped, sin_outer, precision=HIGHEST)
    twist_real = first_real * cos_twist + first_imag * sin_twist
    twist_imag = first_imag * cos_twist - first_real * sin_twist
    spec_real = jnp.einsum("rkb,bq->rkq", twist_real, cos_inner, precision=HIGHEST) + jnp.einsum(
        "rkb,bq->rkq", twist_imag, sin_inner, precision=HIGHEST
    )
    spec_imag = jnp.einsum("rkb,bq->rkq", twist_imag, cos_inner, precision=HIGHEST) - jnp.einsum(
        "rkb,bq->rkq", twist_real, sin_inner, precision=HIGHEST
    )
    return (spec_real, spec_imag)


def inverse_transform(spec_real, spec_imag):
    count, outer, inner = spec_real.shape
    length = outer * inner
    cos_outer, sin_outer = fourier_table(outer)
    cos_inner, sin_inner = fourier_table(inner)
    cos_twist, sin_twist = twiddle_table(outer, inner, length)
    section_real = jnp.einsum("rkq,qm->rkm", spec_real, cos_inner, precision=HIGHEST) - jnp.einsum(
        "rkq,qm->rkm", spec_imag, sin_inner, precision=HIGHEST
    )
    section_imag = jnp.einsum("rkq,qm->rkm", spec_imag, cos_inner, precision=HIGHEST) + jnp.einsum(
        "rkq,qm->rkm", spec_real, sin_inner, precision=HIGHEST
    )
    twist_real = section_real * cos_twist - section_imag * sin_twist
    twist_imag = section_imag * cos_twist + section_real * sin_twist
    result = jnp.einsum("rkm,kj->rjm", twist_real, cos_outer, precision=HIGHEST) - jnp.einsum(
        "rkm,kj->rjm", twist_imag, sin_outer, precision=HIGHEST
    )
    return result.reshape(count, length) / length


def bin_samples(stream, polar_angle, pixel_index, strip_slots, slot_total):
    det_count, total = stream.shape
    strips = strip_slots.shape[1]
    width = total // strips
    sample_slot = jnp.broadcast_to(strip_slots[:, :, None], (det_count, strips, width)).reshape(
        det_count, total
    )
    flat_index = (sample_slot * (3 * TILE_PIX) + pixel_index).reshape(-1)
    values = stream.reshape(-1)
    twice = 2.0 * polar_angle.reshape(-1)
    segment_ids = jnp.concatenate([flat_index, flat_index + TILE_PIX, flat_index + 2 * TILE_PIX])
    payload = jnp.concatenate([values, values * jnp.cos(twice), values * jnp.sin(twice)])
    sums = jax.ops.segment_sum(payload, segment_ids, num_segments=slot_total * 3 * TILE_PIX)
    return sums.reshape(slot_total, 3, TILE_PIX)


def pack_slots(items, target_peer, label, peers, capacity):
    count = target_peer.shape[0]
    counter = jnp.arange(count, dtype=jnp.int32)
    earlier = (target_peer[None, :] == target_peer[:, None]) & (counter[None, :] < counter[:, None])
    rank_in = jnp.sum(earlier.astype(jnp.int32), axis=1)
    target_slot = target_peer * capacity + rank_in
    slot_hits = target_slot[None, :] == jnp.arange(peers * capacity, dtype=jnp.int32)[:, None]
    source_row = jnp.sum(jnp.where(slot_hits, counter[None, :], 0), axis=1)
    filled = jnp.any(slot_hits, axis=1)
    payload = jnp.where(filled[:, None, None], items[source_row], 0.0)
    labels = jnp.where(filled, label[source_row], -1)
    return (payload.reshape(peers, capacity, 3, TILE_PIX), labels.reshape(peers, capacity))


def sum_received(payload, labels, slot_total):
    flat_rows = payload.reshape(-1, 3 * TILE_PIX)
    slot_hits = (
        labels.reshape(-1)[None, :] == jnp.arange(slot_total, dtype=jnp.int32)[:, None]
    ).astype(jnp.float32)
    summed = jnp.dot(slot_hits, flat_rows, precision=HIGHEST, preferred_element_type=jnp.float32)
    return summed.reshape(slot_total, 3, TILE_PIX)


def per_device(
    timestream,
    polar_angle,
    pixel_index,
    strip_tile,
    time_const,
    knee_freq,
    noise_slope,
    white_weight,
    mode_mix,
    coupling,
    device_slots,
    slot_home,
):
    det_count = timestream.shape[1]
    total = timestream.shape[2]
    length = SAMPLES
    scans = total // length
    outer = length // 128
    signal = timestream[0].reshape(det_count * scans, length)
    spec_real, spec_imag = forward_transform(signal)
    positions = jnp.arange(length, dtype=jnp.int32).reshape(128, outer).T
    frequency = ((positions + length // 2) % length - length // 2).astype(jnp.float32) / length
    slope_wide = noise_slope[0][:, None, None]
    power_law = jnp.power(jnp.abs(frequency)[None], slope_wide)
    weight = (
        white_weight[0][:, None, None]
        * power_law
        / (power_law + jnp.power(knee_freq[0][:, None, None], slope_wide))
    )
    lag_phase = 2.0 * math.pi * frequency[None] * time_const[0][:, None, None]
    spec_real = spec_real.reshape(det_count, scans, outer, 128)
    spec_imag = spec_imag.reshape(det_count, scans, outer, 128)
    weight_wide = weight[:, None]
    lag_wide = lag_phase[:, None]
    weighted_real = weight_wide * (spec_real - lag_wide * spec_imag)
    weighted_imag = weight_wide * (spec_imag + lag_wide * spec_real)
    stacked = jnp.stack([weighted_real, weighted_imag], axis=1).reshape(
        det_count, 2 * scans * length
    )
    mixing = mode_mix[0]
    amplitudes = jnp.dot(mixing.T, stacked, precision=HIGHEST, preferred_element_type=jnp.float32)
    summed = lax.psum(amplitudes, "det")
    coupled = jnp.dot(coupling, summed, precision=HIGHEST, preferred_element_type=jnp.float32)
    projected = jnp.dot(
        mixing, coupled, precision=HIGHEST, preferred_element_type=jnp.float32
    ).reshape(det_count, 2, scans, outer, 128)
    cleaned = stacked.reshape(det_count, 2, scans, outer, 128) - weight[:, None, None] * projected
    clean_real = cleaned[:, 0].reshape(det_count * scans, outer, 128)
    clean_imag = cleaned[:, 1].reshape(det_count * scans, outer, 128)
    stream = inverse_transform(clean_real, clean_imag).reshape(det_count, total)
    local_slots = device_slots[0]
    tile_count = local_slots.shape[0]
    gshare = slot_home.shape[1]
    lookup = strip_tile[0][:, :, None] == jnp.arange(tile_count, dtype=jnp.int32)[None, None, :]
    strip_group = jnp.sum(jnp.where(lookup, local_slots[None, None, :], 0), axis=2)
    partials = bin_samples(
        stream, polar_angle[0], pixel_index[0], strip_group, gshare * lax.axis_size("det")
    )
    block_sum = lax.psum_scatter(partials, "det", scatter_dimension=0, tiled=True)
    home_code = slot_home[0]
    owner_payload, owner_labels = pack_slots(
        block_sum, home_code // OWN, home_code % OWN, lax.axis_size("tm"), CAPT
    )
    got_owner, got_places = (
        lax.all_to_all(owner_payload, "tm", split_axis=0, concat_axis=0, tiled=True),
        lax.all_to_all(owner_labels, "tm", split_axis=0, concat_axis=0, tiled=True),
    )
    return sum_received(got_owner, got_places, OWN)


def solution(mesh):
    placed = (
        P("tm", "det", None),
        P("tm", "det", None),
        P("tm", "det", None),
        P("tm", "det", None),
        P("tm", "det"),
        P("tm", "det"),
        P("tm", "det"),
        P("tm", "det"),
        P("tm", "det", None),
        P(),
        P("tm", "det"),
        P("tm", "det"),
    )
    return jax.shard_map(
        per_device,
        mesh=mesh,
        in_specs=placed,
        out_specs=P(("tm", "det"), None, None),
        check_vma=False,
    )
```

profile of v0, /device:TPU:0, one launch (start us, length us, event | category | flops | bytes accessed | tf_op | source)
XLA Modules:
  0.0 2346.8 jit_solution(11479152274990865375)
XLA Ops:
  6.6 1.1 reshape_reshape_squeeze.3
  7.8 0.7 convolution_negate_fusion
  8.4 0.7 fusion.61
  9.1 0.8 fusion.9
  10.0 0.8 fusion.5
  10.8 0.8 convolution_add_fusion.1
  11.7 0.8 convolution_subtract_fusion.2
  13.3 5.7 convolution_bitcast_fusion
  20.5 1.3 pad_add_fusion
  21.8 1.9 cosine_bitcast_fusion
  23.9 109.4 %all-reduce.4.cloned.1.call-done = f32[64,16384]{1,0:T(8,128)} async-done(((f32[64,16384]{1,0:T(8,128)}), f32[64,16384]{1,0:T(8,128)}) %all-reduce.4.cloned.1.call-update) | async-done | bytes 4194320 | tf_op jit(solution)/shard_map/psum | solution.py:155
  133.3 5.6 fusion.140
  138.9 2.3 convolution_bitcast_fusion.1
  141.8 0.8 fusion.32
  142.6 0.8 fusion.30
  143.4 0.8 convolution_subtract_fusion.1
  144.2 0.8 convolution_add_fusion
  145.1 0.7 fusion.14
  145.7 0.7 fusion.2
  146.5 1.3 pad_maximum_fusion
  147.8 2062.8 %scatter_custom_fusion = f32[786432]{0:T(1024)S(1)} fusion(s32[393216]{0:T(1024)} %pad_add_fusion, f32[393216]{0:T(1024)} %pad_maximum_fusion, f32[]{:T(128)} %constant.105.clone.1), kind=kCustom, calls=%fused_computation.6 | custom fusion | flops 393216 | bytes 3146240 | tf_op jit(solution)/shard_map/scatter-add | solution.py:86
  2210.6 3.0 reshape.264
  2215.3 0.7 select_n.143
  2215.9 5.2 all-to-all-start
  2222.4 103.2 %all-reduce.6.cloned.1.call-done = f32[128,3,2048]{2,1,0:T(4,128)} async-done(((f32[128,3,2048]{2,1,0:T(4,128)}), f32[128,3,2048]{2,1,0:T(4,128)}) %all-reduce.6.cloned.1.call-update) | async-done | bytes 3145744
  2325.6 0.9 constant_dynamic-slice_fusion
  2326.6 0.7 gather_fusion.1
  2327.3 0.9 copy_select_fusion
  2328.2 4.2 all-to-all-start.1
  2333.0 0.7 reduce.3
  2333.8 4.9 all-to-all-done.1
  2338.9 1.0 fusion.81
  (63 shorter events, 6.3 us)
Async XLA Ops:
  6.5 126.7 %copy-start = (f32[64,64]{1,0:T(8,128)S(1)}, f32[64,64]{1,0:T(8,128)}, u32[]{:S(2)}) copy-start(f32[64,64]{1,0:T(8,128)} %param.21) | copy-start | bytes 49156
  6.5 126.7 %all-reduce.4.cloned.1.call-start = ((), (), s32[]{:S(2)}) async-start(), calls=%async_computation.2 | async-start | bytes 8388608 | tf_op jit(solution)/shard_map/psum | solution.py:155
  9.9 2.6 copy-start.6
  9.9 2.6 copy-start.9
  9.9 2.6 copy-start.7
  9.9 2.6 copy-start.8
  12.5 0.7 copy-start.3
  19.0 0.7 copy-start.4
  19.0 0.7 copy-start.5
  19.0 1.1 copy-start.2
  19.0 2306.6 %all-reduce.6.cloned.1.call-start = ((), (), s32[]{:S(2)}) async-start(), calls=%async_computation.3 | async-start | bytes 8388608
  20.4 1.5 copy-start.1
  2213.5 0.7 copy-start.10
  2213.6 7.7 copy-start.11
  2215.9 112.3 %all-to-all-start = ((s32[4,1,2]{2,1,0:T(1,128)}), s32[4,1,2]{2,1,0:T(1,128)S(1)}, u32[]{:S(2)}, u32[]{:S(2)}) async-start(s32[4,1,2]{2,1,0:T(1,128)} %bitcast.6), calls=%async_computation | async-start | bytes 4096 | tf_op jit(solution)/shard_map/all_to_all | solution.py:179
  2328.2 10.6 all-to-all-start.1
Sparse Core Ops, SparseCore 0:
  19.1 114.1 all-reduce.3
  2213.7 111.8 all-reduce.5
where the time goes:
time: 2350 us
  other arithmetic  2070 us (88%)
  waiting for transfers between devices  218 us (9%)
  matrix products  23.8 us (1%)
    scatter-add x1, other arithmetic, bin_samples(): jax.ops.segment_sum(payload, segment_ids, num_segments=slot_total * 3 * T...  2060 us
    psum x1, waiting for transfers between devices, per_device(): summed = lax.psum(amplitudes, 'det')  109 us
    unnamed x3, waiting for transfers between devices  103 us
  transfers between devices with their start and end apart: 4, of which 3 were waited for; matrix products, arithmetic and copies ran while one was open for 0% of the time, Pallas kernels for 0%

commit v1 on v0

v1 whole, which is shorter than its diff:
```python
import math

import jax
import jax.numpy as jnp
import numpy as np
from jax import lax
from jax.experimental import pallas as pl
from jax.experimental.pallas import tpu as pltpu
from jax.sharding import PartitionSpec as P

SAMPLES = 4096
OUTER = 32
INNER = 128
DETS = 16
PEERS = 32
STRIPS = 64
MODES = 64
TM = 4
OWN = 8
ROWS = 48

HIGHEST = lax.Precision.HIGHEST
VMEM = pltpu.VMEM
SMEM = pltpu.SMEM


def tables():
    outer = np.arange(OUTER)[:, None]
    inner = np.arange(INNER)[None, :]
    twist = 2.0 * math.pi * outer * inner / SAMPLES
    grid = 2.0 * math.pi * np.outer(np.arange(INNER), np.arange(INNER)) / INNER
    cos_in, sin_in = np.cos(grid), np.sin(grid)
    forward = np.block([[cos_in, -sin_in], [sin_in, cos_in]])
    inverse = np.block([[cos_in, sin_in], [-sin_in, cos_in]]) / SAMPLES
    index = outer + OUTER * inner
    signed = (index + SAMPLES // 2) % SAMPLES - SAMPLES // 2
    freq = signed / SAMPLES
    log_freq = np.where(signed == 0, -1e30, np.log(np.maximum(np.abs(freq), 1e-9)))
    lag = np.where(signed == -(SAMPLES // 2), 0.0, 2.0 * math.pi * freq)
    return [
        np.asarray(t, np.float32)
        for t in (np.cos(twist), np.sin(twist), forward, inverse, log_freq, lag)
    ]


def transform(points, sign):
    count = len(points)
    if count == 1:
        return points
    even = transform(points[0::2], sign)
    odd = transform(points[1::2], sign)
    first, second = [], []
    half = count // 2
    for k in range(half):
        re, im = odd[k]
        angle = sign * 2.0 * math.pi * k / count
        c, s = math.cos(angle), math.sin(angle)
        if k == 0:
            tr, ti = re, im
        elif 4 * k == count:
            tr, ti = (-im, re) if sign > 0 else (im, -re)
        else:
            tr, ti = c * re - s * im, c * im + s * re
        er, ei = even[k]
        first.append((er + tr, ei + ti))
        second.append((er - tr, ei - ti))
    return first + second


def column(row):
    rows = lax.broadcasted_iota(jnp.int32, (DETS, DETS), 0)
    cols = lax.broadcasted_iota(jnp.int32, (DETS, DETS), 1)
    return jnp.sum(jnp.where(rows == cols, row, 0.0), axis=1, keepdims=True)


def forward_kernel(
    slots, signal, tau, knee, slope, white, mix, cos_t, sin_t, matrix, log_f, lag_f,
    out, weight_out, scratch,
):
    for half in range(2):
        lo = 8 * half
        points = [
            (
                signal[lo : lo + 8, a * INNER : (a + 1) * INNER],
                signal[lo : lo + 8, (OUTER + a) * INNER : (OUTER + a + 1) * INNER],
            )
            for a in range(OUTER)
        ]
        for k, (re, im) in enumerate(transform(points, -1)):
            c = cos_t[k : k + 1, :]
            s = sin_t[k : k + 1, :]
            scratch[k * DETS + lo : k * DETS + lo + 8, 0:INNER] = re * c + im * s
            scratch[k * DETS + lo : k * DETS + lo + 8, INNER : 2 * INNER] = im * c - re * s
    tau_c = jnp.broadcast_to(column(tau[...]), (DETS, INNER))
    slope_c = jnp.broadcast_to(column(slope[...]), (DETS, INNER))
    white_c = jnp.broadcast_to(column(white[...]), (DETS, INNER))
    knee_c = jnp.broadcast_to(column(knee[...]), (DETS, INNER))
    knee_p = jnp.exp(slope_c * jnp.log(knee_c))
    group = 8
    for start in range(0, OUTER, group):
        spec = jnp.dot(
            scratch[start * DETS : (start + group) * DETS, :],
            matrix[...],
            precision=HIGHEST,
            preferred_element_type=jnp.float32,
        )
        for step in range(group):
            k = start + step
            power = jnp.exp(slope_c * log_f[k : k + 1, :])
            weight = white_c * power / (power + knee_p)
            lag = tau_c * lag_f[k : k + 1, :]
            re = spec[step * DETS : (step + 1) * DETS, 0:INNER]
            im = spec[step * DETS : (step + 1) * DETS, INNER : 2 * INNER]
            weight_out[k] = weight
            out[k, 0:DETS, :] = weight * (re - lag * im)
            out[k, DETS : 2 * DETS, :] = weight * (im + lag * re)
    mixed = jnp.concatenate([mix[0:8, :], mix[8:16, :]], axis=1)
    for k in range(OUTER):
        out[k, 32:40, :] = mixed
        out[k, 40:48, :] = jnp.full((8, INNER), -1.0, jnp.float32)

    def mark(entry, carry):
        slot = slots[0, entry]
        block = slot // 4

        def earlier(other, rank):
            return rank + jnp.where(slots[0, other] // 4 == block, 1, 0)

        rank = lax.fori_loop(0, entry, earlier, 0)
        rows = lax.broadcasted_iota(jnp.int32, (8, INNER), 0)
        value = (slot - 4 * block).astype(jnp.float32)
        old = out[block, 40:48, :]
        out[block, 40:48, :] = jnp.where(rows == rank, value, old)
        return carry

    lax.fori_loop(0, PEERS, mark, 0)


def couple_kernel(got, coupling, out, labels):
    amps = None
    mixes = []
    for half in range(2):
        lo = 8 * half
        re = got[:, lo : lo + 8, :].reshape(PEERS * 8, INNER)
        im = got[:, DETS + lo : DETS + lo + 8, :].reshape(PEERS * 8, INNER)
        mix = got[:, 32:40, half * MODES : (half + 1) * MODES].reshape(PEERS * 8, MODES)
        both = jnp.concatenate([re, im], axis=1)
        part = lax.dot_general(
            mix, both, (((0,), (0,)), ((), ())),
            precision=HIGHEST, preferred_element_type=jnp.float32,
        )
        amps = part if amps is None else amps + part
        mixes.append(mix)
    coupled = jnp.dot(
        coupling[...], amps, precision=HIGHEST, preferred_element_type=jnp.float32
    )
    for half in range(2):
        lo = 8 * half
        back = jnp.dot(
            mixes[half], coupled, precision=HIGHEST, preferred_element_type=jnp.float32
        )
        out[:, lo : lo + 8, :] = back[:, 0:INNER].reshape(PEERS, 8, INNER)
        out[:, DETS + lo : DETS + lo + 8, :] = back[:, INNER:].reshape(PEERS, 8, INNER)
    labels[...] = got[:, 40:48, :]


def bin_kernel(
    slots, tiles, weighted, weight, back, cosine, sine, pixel, cos_t, sin_t, matrix,
    out, scratch, stream, send_slot,
):
    for k in range(OUTER):
        re = weighted[k, 0:DETS, :] - weight[k] * back[k, 0:DETS, :]
        im = weighted[k, DETS : 2 * DETS, :] - weight[k] * back[k, DETS : 2 * DETS, :]
        scratch[k * DETS : (k + 1) * DETS, 0:INNER] = re
        scratch[k * DETS : (k + 1) * DETS, INNER : 2 * INNER] = im
    group = 8
    for start in range(0, OUTER, group):
        section = jnp.dot(
            scratch[start * DETS : (start + group) * DETS, :],
            matrix[...],
            precision=HIGHEST,
            preferred_element_type=jnp.float32,
        )
        for step in range(group):
            k = start + step
            c = cos_t[k : k + 1, :]
            s = sin_t[k : k + 1, :]
            re = section[step * DETS : (step + 1) * DETS, 0:INNER]
            im = section[step * DETS : (step + 1) * DETS, INNER : 2 * INNER]
            scratch[k * DETS : (k + 1) * DETS, 0:INNER] = re * c - im * s
            scratch[k * DETS : (k + 1) * DETS, INNER : 2 * INNER] = im * c + re * s
    for half in range(2):
        lo = 8 * half
        points = [
            (
                scratch[k * DETS + lo : k * DETS + lo + 8, 0:INNER],
                scratch[k * DETS + lo : k * DETS + lo + 8, INNER : 2 * INNER],
            )
            for k in range(OUTER)
        ]
        for a, (re, im) in enumerate(transform(points, 1)):
            stream[a, lo : lo + 8, :] = re
            stream[OUTER + a, lo : lo + 8, :] = im

    def assign(entry, carry):
        block = slots[0, entry] // 4

        def earlier(other, rank):
            return rank + jnp.where(slots[0, other] // 4 == block, 1, 0)

        send_slot[entry] = 2 * block + lax.fori_loop(0, entry, earlier, 0)
        return carry

    lax.fori_loop(0, PEERS, assign, 0)

    def clear(entry, carry):
        out[entry] = jnp.zeros((ROWS, INNER), jnp.float32)
        return carry

    lax.fori_loop(0, 2 * PEERS, clear, 0)
    lanes = lax.broadcasted_iota(jnp.int32, (16, INNER), 0).astype(jnp.float32)
    marks = [(lanes + 16.0 * g).astype(jnp.bfloat16) for g in range(8)]
    one = jnp.ones((16, INNER), jnp.bfloat16)
    zero = jnp.zeros((16, INNER), jnp.bfloat16)

    def strip(s, carry):
        base = pl.multiple_of(s * INNER, INNER)
        pix = pixel[:, pl.ds(base, INNER)]
        high = (pix >> 7).astype(jnp.float32)
        low = (pix & 127).astype(jnp.float32)
        values = stream[s]
        maps = [values, values * cosine[:, pl.ds(base, INNER)], values * sine[:, pl.ds(base, INNER)]]
        tops = [m.astype(jnp.bfloat16).astype(jnp.float32) for m in maps]
        rests = [m - t for m, t in zip(maps, tops)]
        parts = tops + rests

        def spread(block, d):
            return jnp.broadcast_to(block[d : d + 1, :], (16, INNER)).astype(jnp.bfloat16)

        for d in range(DETS):
            high_d = spread(high, d)
            low_d = spread(low, d)
            hit = high_d == marks[0]
            left = jnp.concatenate(
                [jnp.where(hit, spread(p, d), zero) for p in parts], axis=0
            )
            right = jnp.concatenate(
                [jnp.where(low_d == marks[g], one, zero) for g in range(8)], axis=0
            )
            sums = lax.dot_general(
                left, right, (((1,), (1,)), ((), ())), preferred_element_type=jnp.float32
            )
            slot = send_slot[tiles[d, s]]
            out[slot] = out[slot] + (sums[0:ROWS, :] + sums[ROWS:, :])
        return carry

    lax.fori_loop(0, STRIPS, strip, 0)


def gather_kernel(homes, got, labels, out):
    for place in range(2 * TM):
        out[place, 0:ROWS, :] = jnp.zeros((ROWS, INNER), jnp.float32)
        out[place, ROWS:, :] = jnp.full((8, INNER), -1.0, jnp.float32)
    for tile in range(4):
        def add(source, total):
            for rank in range(2):
                hit = labels[source, rank : rank + 1, :] == float(tile)
                total = total + jnp.where(
                    hit, got[source, rank * ROWS : (rank + 1) * ROWS, :], 0.0
                )
            return total

        total = lax.fori_loop(
            0, PEERS, add, jnp.zeros((ROWS, INNER), jnp.float32), unroll=4
        )
        owner = homes[0, tile] // OWN
        rank = 0
        for other in range(tile):
            rank = rank + jnp.where(homes[0, other] // OWN == owner, 1, 0)
        row = 2 * owner + rank
        out[row, 0:ROWS, :] = total
        place = (homes[0, tile] - OWN * owner).astype(jnp.float32)
        out[row, ROWS:, :] = jnp.broadcast_to(place, (8, INNER))


def place_kernel(got, out):
    for place in range(OWN):
        total = jnp.zeros((ROWS, INNER), jnp.float32)
        for source in range(2 * TM):
            hit = got[source, ROWS : ROWS + 1, :] == float(place)
            total = total + jnp.where(hit, got[source, 0:ROWS, :], 0.0)
        out[place] = total


def call(kernel, outs, specs, *operands, scratch=()):
    return pl.pallas_call(
        kernel,
        out_shape=outs,
        in_specs=[pl.BlockSpec(memory_space=s) for s in specs],
        scratch_shapes=list(scratch),
        compiler_params=pltpu.CompilerParams(vmem_limit_bytes=48 << 20),
    )(*operands)


def per_device(
    timestream, polar_angle, pixel_index, strip_tile, time_const, knee_freq, noise_slope,
    white_weight, mode_mix, coupling, device_slots, slot_home,
):
    f32 = jnp.float32
    cos_t, sin_t, forward, inverse, log_f, lag_f = [jnp.asarray(t) for t in tables()]
    packed, weight = call(
        forward_kernel,
        (
            jax.ShapeDtypeStruct((PEERS, 48, INNER), f32),
            jax.ShapeDtypeStruct((PEERS, DETS, INNER), f32),
        ),
        [SMEM] + [VMEM] * 11,
        device_slots, timestream[0], time_const, knee_freq, noise_slope, white_weight,
        mode_mix[0], cos_t, sin_t, forward, log_f, lag_f,
        scratch=[VMEM((OUTER * DETS, 2 * INNER), f32)],
    )
    got = lax.all_to_all(packed, "det", 0, 0, tiled=True)
    projected, labels = call(
        couple_kernel,
        (
            jax.ShapeDtypeStruct((PEERS, 2 * DETS, INNER), f32),
            jax.ShapeDtypeStruct((PEERS, 8, INNER), f32),
        ),
        [VMEM] * 2,
        got, coupling,
    )
    back = lax.all_to_all(projected, "det", 0, 0, tiled=True)
    twice = 2.0 * polar_angle[0]
    partials = call(
        bin_kernel,
        jax.ShapeDtypeStruct((2 * PEERS, ROWS, INNER), f32),
        [SMEM] * 2 + [VMEM] * 9,
        device_slots, strip_tile[0], packed, weight, back, jnp.cos(twice), jnp.sin(twice),
        pixel_index[0], cos_t, sin_t, inverse,
        scratch=[
            VMEM((OUTER * DETS, 2 * INNER), f32),
            VMEM((STRIPS, DETS, INNER), f32),
            SMEM((PEERS,), jnp.int32),
        ],
    )
    parts = lax.all_to_all(
        partials.reshape(PEERS, 2 * ROWS, INNER), "det", 0, 0, tiled=True
    )
    owned = call(
        gather_kernel,
        jax.ShapeDtypeStruct((2 * TM, ROWS + 8, INNER), f32),
        [SMEM] + [VMEM] * 2,
        slot_home, parts, labels,
    )
    final = lax.all_to_all(
        owned.reshape(TM, 2 * (ROWS + 8), INNER), "tm", 0, 0, tiled=True
    )
    placed = call(
        place_kernel,
        jax.ShapeDtypeStruct((OWN, ROWS, INNER), f32),
        [VMEM],
        final.reshape(2 * TM, ROWS + 8, INNER),
    )
    return placed.reshape(OWN, 3, 16 * INNER)


def solution(mesh):
    strips = P("tm", "det", None)
    dets = P("tm", "det")
    return jax.shard_map(
        per_device,
        mesh=mesh,
        in_specs=(strips,) * 4 + (dets,) * 4 + (strips, P(), dets, dets),
        out_specs=P(("tm", "det"), None, None),
        check_vma=False,
    )
```

time: 2350 us -> 138 us (0.06)
  other arithmetic: 2070 us -> 2.81 us
  waiting for transfers between devices: 218 us -> 8.77 us
  blocking collectives: 0 us -> 59.7 us
  Pallas kernels: 0 us -> 50.3 us
  matrix products: 23.8 us -> 0 us
    scatter-add x1 -> x0, other arithmetic: 2060 us -> none  [bin_samples(): jax.ops.segment_sum(payload, segment_ids, num_segments=slot_total * 3 * T...]
    psum x1 -> x0, waiting for transfers between devices: 109 us -> none  [per_device(): summed = lax.psum(amplitudes, 'det')]
    unnamed x3 -> x0, waiting for transfers between devices: 103 us -> none
    all_to_all x0 -> x3, blocking collectives: none -> 59.7 us  [the longest x1 26.3 us: per_device(): lax.all_to_all(partials.reshape(PEERS, 2 * ROWS, INNER), 'det', 0, 0, til...]
    pallas_call x0 -> x5, Pallas kernels: none -> 50.3 us  [call(): pl.pallas_call(kernel, out_shape=outs, in_specs=[pl.BlockSpec(memory_spac...]
    dot_general x16 -> x0, matrix products: 23.8 us -> none  [the longest x1 5.72 us: per_device(): jnp.dot(mixing.T, stacked, precision=HIGHEST, preferred_element_type=jnp....]
  transfers between devices with their start and end apart: 4 -> 1, of which waited for: 3 -> 1; matrix products, arithmetic and copies ran while one was open for 0% -> 2% of each run, Pallas kernels for 0% -> 0%
where the time goes in v1:
time: 138 us; the launch traced here: 137 us
  blocking collectives  59.7 us (43%)
  Pallas kernels  50.3 us (36%)
  local copies, waits for them, and re-layouts  11.8 us (9%)
  waiting for transfers between devices  8.77 us (6%)
  starting transfers between devices  3.89 us (3%)
  other arithmetic  2.81 us (2%)
    pallas_call x5, Pallas kernels, call(): pl.pallas_call(kernel, out_shape=outs, in_specs=[pl.BlockSpec(memory_spac...  50.3 us
    all_to_all x1, blocking collectives, per_device(): lax.all_to_all(partials.reshape(PEERS, 2 * ROWS, INNER), 'det', 0, 0, til...  26.3 us
    all_to_all x1, blocking collectives, per_device(): got = lax.all_to_all(packed, 'det', 0, 0, tiled=True)  22.8 us
    unnamed x40, local copies, waits for them, and re-layouts  10.9 us
    all_to_all x1, blocking collectives, per_device(): lax.all_to_all(owned.reshape(TM, 2 * (ROWS + 8), INNER), 'tm', 0, 0, tile...  10.7 us
    all_to_all x1, waiting for transfers between devices, per_device(): back = lax.all_to_all(projected, 'det', 0, 0, tiled=True)  8.77 us
    all_to_all x1, starting transfers between devices, per_device(): back = lax.all_to_all(projected, 'det', 0, 0, tiled=True)  3.89 us
    sin x1, other arithmetic, per_device(): jnp.sin(twice)  2.81 us
  transfers between devices with their start and end apart: 1, of which 1 were waited for; matrix products, arithmetic and copies ran while one was open for 2% of the time, Pallas kernels for 0%

profile of v1, /device:TPU:0, one launch (start us, length us, event | category | flops | bytes accessed | tf_op | source)
XLA Modules:
  0.0 137.4 jit_solution(1056309234901801939)
XLA Ops:
  0.0 1.0 copy-done
  1.0 0.9 copy-done.2
  2.0 0.7 copy-done.4
  2.7 0.7 copy-done.6
  3.4 0.7 copy-done.9
  4.1 0.7 copy-done.10
  4.9 0.7 copy-done.11
  5.6 0.7 copy-done.13
  6.2 0.7 copy-done.15
  6.9 0.7 copy-done.16
  7.5 0.7 copy-done.17
  8.2 0.7 copy-done.18
  8.8 7.9 %shard_map.172 = (f32[32,48,128]{2,1,0:T(8,128)S(1)}, f32[32,16,128]{2,1,0:T(8,128)S(1)}) custom-call(s32[1,32]{1,0:T(1,128)S(1)} %copy-done.13, f32[16,8192]{1,0:T(8,128)S(1)} %bitcast.14, f32[1,16]{1,0:T(1,128)S(1)} %copy-done.15, f32[1,16]{1,0:T(1,128)S(1)} %copy-done.16, f32[1,16]{1,0:T(1,128)S(1)} %copy-done.17, f32[1,16]{1,0:T(1,128)S(1)} %copy-done.18, ...), custom_call_target="tpu_custom_call" | custom-call | tf_op jit(solution)/shard_map/pallas_call | solution.py:296
  16.7 22.8 %all_to_all.20.got = f32[32,48,128]{2,1,0:T(8,128)S(1)} all-to-all(f32[32,48,128]{2,1,0:T(8,128)S(1)} %get-tuple-element.9.weighted), channel_id=1, replica_groups=mesh['tm'=4,'det'=32] {'det'}, dimensions={0} | all-to-all | bytes 1572864 | tf_op jit(solution)/shard_map/all_to_all | solution.py:322
  39.5 0.0 copy-done.8
  39.5 2.4 %shard_map.173 = (f32[32,32,128]{2,1,0:T(8,128)}, f32[32,8,128]{2,1,0:T(8,128)S(1)}) custom-call(f32[32,48,128]{2,1,0:T(8,128)S(1)} %all_to_all.20.got, f32[64,64]{1,0:T(8,128)S(1)} %copy-done.8), custom_call_target="tpu_custom_call" | custom-call | tf_op jit(solution)/shard_map/pallas_call | solution.py:296
  41.9 3.9 %all-to-all-start.1 = ((f32[32,32,128]{2,1,0:T(8,128)}), f32[32,32,128]{2,1,0:T(8,128)S(1)}, u32[]{:S(2)}, u32[]{:S(2)}) async-start(f32[32,32,128]{2,1,0:T(8,128)} %get-tuple-element.11), calls=%async_computation.1 | async-start | bytes 1048576 | tf_op jit(solution)/shard_map/all_to_all | solution.py:332
  45.8 2.8 %sine_bitcast_fusion = (f32[16,8192]{1,0:T(8,128)S(1)}, f32[16,8192]{1,0:T(8,128)S(1)}) fusion(f32[1,16,8192]{2,1,0:T(8,128)} %param.19), kind=kLoop, calls=%fused_computation | loop fusion | flops 131072 | bytes 1572864 | tf_op jit(solution)/shard_map/sin | solution.py:338
  48.6 8.8 %all-to-all-done.1.back = f32[32,32,128]{2,1,0:T(8,128)S(1)} async-done(((f32[32,32,128]{2,1,0:T(8,128)}), f32[32,32,128]{2,1,0:T(8,128)S(1)}, u32[]{:S(2)}, u32[]{:S(2)}) %all-to-all-start.1) | async-done | bytes 524320 | tf_op jit(solution)/shard_map/all_to_all | solution.py:332
  57.4 0.0 copy-done.3
  57.4 0.0 copy-start.7
  57.4 0.7 copy-done.7
  58.1 0.7 copy-done.12
  58.8 0.7 copy-done.14
  59.5 38.6 %shard_map.174 = f32[64,48,128]{2,1,0:T(8,128)S(1)} custom-call(s32[1,32]{1,0:T(1,128)S(1)} %copy-done.14, s32[16,64]{1,0:T(8,128)S(1)} %bitcast.17, f32[32,48,128]{2,1,0:T(8,128)S(1)} %get-tuple-element.9.weighted, f32[32,16,128]{2,1,0:T(8,128)S(1)} %get-tuple-element.10.weight, f32[32,32,128]{2,1,0:T(8,128)S(1)} %all-to-all-done.1.back, ...), custom_call_target="tpu_custom_call" | custom-call | tf_op jit(solution)/shard_map/pallas_call | solution.py:296
  98.1 0.0 copy-start.19
  98.1 26.3 %all_to_all.21.got = f32[32,96,128]{2,1,0:T(8,128)S(1)} all-to-all(f32[32,96,128]{2,1,0:T(8,128)S(1)} %bitcast.11), channel_id=1, replica_groups=mesh['tm'=4,'det'=32] {'det'}, dimensions={0} | all-to-all | bytes 3145728 | tf_op jit(solution)/shard_map/all_to_all | solution.py:346
  124.4 1.3 shard_map.175
  125.7 10.7 %all_to_all.22 = f32[4,112,128]{2,1,0:T(8,128)S(1)} all-to-all(f32[4,112,128]{2,1,0:T(8,128)S(1)} %bitcast.13), channel_id=1, replica_groups=mesh['tm'=4,'det'=32] {'tm'}, dimensions={0} | all-to-all | bytes 458752 | tf_op jit(solution)/shard_map/all_to_all | solution.py:355
  136.4 0.1 shard_map.176
  136.5 0.1 reshape.19
  136.6 0.8 copy.20
  (21 shorter events, 0.0 us)
Async XLA Ops:
  0.0 1.0 copy-start
  1.0 0.9 copy-start.2
  2.0 0.7 copy-start.4
  2.7 0.7 copy-start.6
  3.4 0.7 copy-start.9
  4.1 0.7 copy-start.10
  4.9 0.7 copy-start.11
  5.6 0.7 copy-start.13
  6.2 0.7 copy-start.15
  6.9 0.7 copy-start.16
  7.5 0.7 copy-start.17
  8.2 0.7 copy-start.18
  8.8 30.7 %copy-start.8 = (f32[64,64]{1,0:T(8,128)S(1)}, f32[64,64]{1,0:T(8,128)}, u32[]{:S(2)}) copy-start(f32[64,64]{1,0:T(8,128)} %coupling.1) | copy-start | bytes 49156
  39.5 17.9 %copy-start.1 = (s32[1,16,8192]{2,1,0:T(8,128)S(1)}, s32[1,16,8192]{2,1,0:T(8,128)}, u32[]{:S(2)}) copy-start(s32[1,16,8192]{2,1,0:T(8,128)} %param.20) | copy-start | bytes 1572868
  39.5 17.9 %copy-start.3 = (f32[256,256]{1,0:T(8,128)S(1)}, f32[256,256]{1,0:T(8,128)}, u32[]{:S(2)}) copy-start(f32[256,256]{1,0:T(8,128)} %constant.17.clone.matrix) | copy-start | bytes 786436
  39.5 17.9 %copy-start.5 = (f32[32,128]{1,0:T(8,128)S(1)}, f32[32,128]{1,0:T(8,128)}, u32[]{:S(2)}) copy-start(f32[32,128]{1,0:T(8,128)} %constant.15.clone.sin_t) | copy-start | bytes 49156
  41.9 15.5 %all-to-all-start.1 = ((f32[32,32,128]{2,1,0:T(8,128)}), f32[32,32,128]{2,1,0:T(8,128)S(1)}, u32[]{:S(2)}, u32[]{:S(2)}) async-start(f32[32,32,128]{2,1,0:T(8,128)} %get-tuple-element.11), calls=%async_computation.1 | async-start | bytes 1048576 | tf_op jit(solution)/shard_map/all_to_all | solution.py:332
  57.4 0.7 copy-start.7
  58.1 0.7 copy-start.12
  58.8 0.7 copy-start.14
  98.1 26.3 %copy-start.19 = (s32[1,4]{1,0:T(1,128)S(1)}, s32[1,4]{1,0:T(1,128)}, u32[]{:S(2)}) copy-start(s32[1,4]{1,0:T(1,128)} %homes.1) | copy-start | bytes 52

commit v2 on v1

v2 whole, which is shorter than its diff:
```python
import math

import jax
import jax.numpy as jnp
import numpy as np
from jax import lax
from jax.experimental import pallas as pl
from jax.experimental.pallas import tpu as pltpu
from jax.sharding import PartitionSpec as P

SAMPLES = 4096
OUTER = 32
INNER = 128
DETS = 16
PEERS = 32
STRIPS = 64
MODES = 64
TM = 4
OWN = 8
UNROLL = 4
ROWS = 48

HIGHEST = lax.Precision.HIGHEST
VMEM = pltpu.VMEM
SMEM = pltpu.SMEM
HBM = pltpu.HBM


def tables():
    outer = np.arange(OUTER)[:, None]
    inner = np.arange(INNER)[None, :]
    twist = 2.0 * math.pi * outer * inner / SAMPLES
    grid = 2.0 * math.pi * np.outer(np.arange(INNER), np.arange(INNER)) / INNER
    cos_in, sin_in = np.cos(grid), np.sin(grid)
    forward = np.block([[cos_in, -sin_in], [sin_in, cos_in]])
    inverse = np.block([[cos_in, sin_in], [-sin_in, cos_in]]) / SAMPLES
    index = outer + OUTER * inner
    signed = (index + SAMPLES // 2) % SAMPLES - SAMPLES // 2
    freq = signed / SAMPLES
    log_freq = np.where(signed == 0, -1e30, np.log(np.maximum(np.abs(freq), 1e-9)))
    lag = np.where(signed == -(SAMPLES // 2), 0.0, 2.0 * math.pi * freq)
    rows = np.concatenate([np.cos(twist), np.sin(twist), log_freq, lag], axis=0)
    rows, forward, inverse = [np.asarray(t, np.float32) for t in (rows, forward, inverse)]
    top = inverse.astype(jnp.bfloat16)
    rest = (inverse - top.astype(np.float32)).astype(jnp.bfloat16)
    return rows, forward, np.stack([top, rest])


def transform(points, sign):
    count = len(points)
    if count == 1:
        return points
    even = transform(points[0::2], sign)
    odd = transform(points[1::2], sign)
    first, second = [], []
    half = count // 2
    for k in range(half):
        re, im = odd[k]
        angle = sign * 2.0 * math.pi * k / count
        c, s = math.cos(angle), math.sin(angle)
        if k == 0:
            tr, ti = re, im
        elif 4 * k == count:
            tr, ti = (-im, re) if sign > 0 else (im, -re)
        else:
            tr, ti = c * re - s * im, c * im + s * re
        er, ei = even[k]
        first.append((er + tr, ei + ti))
        second.append((er - tr, ei - ti))
    return first + second


def split(x):
    top = x.astype(jnp.bfloat16)
    return top, (x - top.astype(jnp.float32)).astype(jnp.bfloat16)


def product(left, right, dims=(((1,), (0,)), ((), ()))):
    def dot(a, b):
        return lax.dot_general(a, b, dims, preferred_element_type=jnp.float32)

    return dot(left[0], right[0]) + (dot(left[0], right[1]) + dot(left[1], right[0]))


def column(row):
    rows = lax.broadcasted_iota(jnp.int32, (DETS, DETS), 0)
    cols = lax.broadcasted_iota(jnp.int32, (DETS, DETS), 1)
    return jnp.sum(jnp.where(rows == cols, row, 0.0), axis=1, keepdims=True)


def ranks(slots, counts, mark):
    for block in range(PEERS):
        counts[block] = 0
    for entry in range(PEERS):
        slot = slots[0, entry]
        block = slot >> 2
        rank = counts[block]
        counts[block] = rank + 1
        mark(entry, slot, block, rank)


def forward_kernel(
    slots_h, signal_h, tau_h, knee_h, slope_h, white_h, mix_h, rows_h, matrix_h,
    out, weight_out, scratch, slots, signal, tau, knee, slope, white, mix, rows, matrix,
    counts, sems,
):
    pairs = [
        (signal_h.at[0], signal), (rows_h, rows), (slots_h, slots), (tau_h, tau),
        (knee_h, knee), (slope_h, slope), (white_h, white), (mix_h.at[0], mix),
        (matrix_h, matrix),
    ]
    copies = [pltpu.make_async_copy(a, b, sems.at[i]) for i, (a, b) in enumerate(pairs)]
    for copy in copies:
        copy.start()
    for copy in copies[2:8]:
        copy.wait()
    mixed = jnp.concatenate([mix[0:8, :], mix[8:16, :]], axis=1)
    for k in range(OUTER):
        out[k, 32:40, :] = mixed
        out[k, 40:48, :] = jnp.full((8, INNER), -1.0, jnp.float32)

    def mark(entry, slot, block, rank):
        value = (slot - 4 * block).astype(jnp.float32)
        out[block, pl.ds(40 + rank, 1), :] = jnp.broadcast_to(value, (1, INNER))

    ranks(slots, counts, mark)
    for copy in copies[0:2]:
        copy.wait()
    for half in range(2):
        lo = 8 * half
        points = [
            (
                signal[lo : lo + 8, a * INNER : (a + 1) * INNER],
                signal[lo : lo + 8, (OUTER + a) * INNER : (OUTER + a + 1) * INNER],
            )
            for a in range(OUTER)
        ]
        for k, (re, im) in enumerate(transform(points, -1)):
            c = rows[k : k + 1, :]
            s = rows[OUTER + k : OUTER + k + 1, :]
            scratch[k * DETS + lo : k * DETS + lo + 8, 0:INNER] = re * c + im * s
            scratch[k * DETS + lo : k * DETS + lo + 8, INNER : 2 * INNER] = im * c - re * s
    tau_c = jnp.broadcast_to(column(tau[...]), (DETS, INNER))
    slope_c = jnp.broadcast_to(column(slope[...]), (DETS, INNER))
    white_c = jnp.broadcast_to(column(white[...]), (DETS, INNER))
    knee_c = jnp.broadcast_to(column(knee[...]), (DETS, INNER))
    knee_p = jnp.exp(slope_c * jnp.log(knee_c))
    copies[8].wait()
    group = 8
    for start in range(0, OUTER, group):
        spec = jnp.dot(
            scratch[start * DETS : (start + group) * DETS, :],
            matrix[...],
            precision=HIGHEST,
            preferred_element_type=jnp.float32,
        )
        for step in range(group):
            k = start + step
            power = jnp.exp(slope_c * rows[2 * OUTER + k : 2 * OUTER + k + 1, :])
            weight = white_c * power / (power + knee_p)
            lag = tau_c * rows[3 * OUTER + k : 3 * OUTER + k + 1, :]
            re = spec[step * DETS : (step + 1) * DETS, 0:INNER]
            im = spec[step * DETS : (step + 1) * DETS, INNER : 2 * INNER]
            weight_out[k] = weight
            out[k, 0:DETS, :] = weight * (re - lag * im)
            out[k, DETS : 2 * DETS, :] = weight * (im + lag * re)


def couple_kernel(got, coupling_h, out, labels, coupling, sem):
    copy = pltpu.make_async_copy(coupling_h, coupling, sem)
    copy.start()
    amps = None
    mixes = []
    for half in range(2):
        lo = 8 * half
        re = got[:, lo : lo + 8, :].reshape(PEERS * 8, INNER)
        im = got[:, DETS + lo : DETS + lo + 8, :].reshape(PEERS * 8, INNER)
        mix = split(
            got[:, 32:40, half * MODES : (half + 1) * MODES].reshape(PEERS * 8, MODES)
        )
        both = split(jnp.concatenate([re, im], axis=1))
        part = product(mix, both, (((0,), (0,)), ((), ())))
        amps = part if amps is None else amps + part
        mixes.append(mix)
    copy.wait()
    coupled = split(product(split(coupling[...]), split(amps)))
    for half in range(2):
        lo = 8 * half
        back = product(mixes[half], coupled)
        out[:, lo : lo + 8, :] = back[:, 0:INNER].reshape(PEERS, 8, INNER)
        out[:, DETS + lo : DETS + lo + 8, :] = back[:, INNER:].reshape(PEERS, 8, INNER)
    labels[...] = got[:, 40:48, :]


def bin_kernel(
    slots_h, tiles_h, weighted, weight, back, cosine, sine, pixel_h, rows_h, matrix_h,
    out, scratch, stream, slots, tiles, pixel, rows, matrix, counts, parts,
    even, odd, sems,
):
    pairs = [
        (matrix_h, matrix), (rows_h, rows), (slots_h, slots), (tiles_h.at[0], tiles),
        (pixel_h.at[0], pixel),
    ]
    copies = [pltpu.make_async_copy(a, b, sems.at[i]) for i, (a, b) in enumerate(pairs)]
    for copy in copies:
        copy.start()
    for k in range(OUTER):
        re = weighted[k, 0:DETS, :] - weight[k] * back[k, 0:DETS, :]
        im = weighted[k, DETS : 2 * DETS, :] - weight[k] * back[k, DETS : 2 * DETS, :]
        scratch[k * DETS : (k + 1) * DETS, 0:INNER] = re
        scratch[k * DETS : (k + 1) * DETS, INNER : 2 * INNER] = im
    for copy in copies[0:2]:
        copy.wait()
    group = 8
    for start in range(0, OUTER, group):
        section = product(
            split(scratch[start * DETS : (start + group) * DETS, :]), (matrix[0], matrix[1])
        )
        for step in range(group):
            k = start + step
            c = rows[k : k + 1, :]
            s = rows[OUTER + k : OUTER + k + 1, :]
            re = section[step * DETS : (step + 1) * DETS, 0:INNER]
            im = section[step * DETS : (step + 1) * DETS, INNER : 2 * INNER]
            scratch[k * DETS : (k + 1) * DETS, 0:INNER] = re * c - im * s
            scratch[k * DETS : (k + 1) * DETS, INNER : 2 * INNER] = im * c + re * s
    for half in range(2):
        lo = 8 * half
        points = [
            (
                scratch[k * DETS + lo : k * DETS + lo + 8, 0:INNER],
                scratch[k * DETS + lo : k * DETS + lo + 8, INNER : 2 * INNER],
            )
            for k in range(OUTER)
        ]
        for a, (re, im) in enumerate(transform(points, 1)):
            stream[a, lo : lo + 8, :] = re
            stream[OUTER + a, lo : lo + 8, :] = im

    def clear(entry, carry):
        blank = jnp.zeros((ROWS, INNER), jnp.float32)
        even[entry] = jnp.zeros((2 * ROWS, INNER // 2), jnp.float32)
        odd[entry] = jnp.zeros((2 * ROWS, INNER // 2), jnp.float32)
        out[entry] = blank
        out[PEERS + entry] = blank
        return carry

    lax.fori_loop(0, PEERS, clear, 0)
    for copy in copies[2:]:
        copy.wait()
    levels = lax.broadcasted_iota(jnp.int32, (16, INNER), 0).astype(jnp.float32)
    marks = [(levels + 16.0 * g).astype(jnp.bfloat16) for g in range(8)]
    one = jnp.ones((16, INNER), jnp.bfloat16)
    zero = jnp.zeros((16, INNER), jnp.bfloat16)

    def block(start, carry):
        for step in range(UNROLL):
            s = start * UNROLL + step
            base = pl.multiple_of(s * INNER, INNER)
            pix = pixel[:, pl.ds(base, INNER)]
            values = stream[s]
            maps = [
                values,
                values * cosine[:, pl.ds(base, INNER)],
                values * sine[:, pl.ds(base, INNER)],
            ]
            tops = [m.astype(jnp.bfloat16).astype(jnp.float32) for m in maps]
            rests = [m - t for m, t in zip(maps, tops)]
            fields = [
                ((pix >> 7) + 16 * ((pix >> 6) & 1)).astype(jnp.float32),
                (pix & 63).astype(jnp.float32),
            ]
            for i, field in enumerate(fields + tops + rests):
                at = (step * 8 + i) * DETS
                parts[at : at + DETS, :] = field
        for step in range(UNROLL):
            s = start * UNROLL + step

            def spread(i, d):
                row = (step * 8 + i) * DETS + d
                wide = parts[pl.ds(row, 8, stride=0), :]
                return jnp.concatenate([wide, wide], axis=0).astype(jnp.bfloat16)

            for d in range(DETS):
                low_d = spread(1, d)
                high_d = spread(0, d)
                hits = [high_d == marks[0], high_d == marks[1]]
                left = []
                for c in range(6):
                    value = spread(2 + c, d)
                    left += [jnp.where(hit, value, zero) for hit in hits]
                left = jnp.concatenate(left, axis=0)
                right = jnp.concatenate(
                    [jnp.where(low_d == marks[g], one, zero) for g in range(4)], axis=0
                )
                sums = lax.dot_general(
                    left, right, (((1,), (1,)), ((), ())), preferred_element_type=jnp.float32
                )
                tile = tiles[d, s]
                total = (even, odd)[d % 2]
                total[tile] = total[tile] + (sums[0 : 2 * ROWS, :] + sums[2 * ROWS :, :])
        return carry

    lax.fori_loop(0, STRIPS // UNROLL, block, 0)

    def settle(entry, slot, home, rank):
        both = even[entry] + odd[entry]
        for c in range(3):
            out[2 * home + rank, 16 * c : 16 * c + 16, :] = jnp.concatenate(
                [both[32 * c : 32 * c + 16, :], both[32 * c + 16 : 32 * c + 32, :]], axis=1
            )

    ranks(slots, counts, settle)


def gather_kernel(homes, got, labels, out):
    for place in range(2 * TM):
        out[place, 0:ROWS, :] = jnp.zeros((ROWS, INNER), jnp.float32)
        out[place, ROWS:, :] = jnp.full((8, INNER), -1.0, jnp.float32)
    for tile in range(4):
        def add(source, total):
            for rank in range(2):
                hit = labels[source, rank : rank + 1, :] == float(tile)
                total = total + jnp.where(
                    hit, got[source, rank * ROWS : (rank + 1) * ROWS, :], 0.0
                )
            return total

        total = lax.fori_loop(
            0, PEERS, add, jnp.zeros((ROWS, INNER), jnp.float32), unroll=4
        )
        owner = homes[0, tile] // OWN
        rank = 0
        for other in range(tile):
            rank = rank + jnp.where(homes[0, other] // OWN == owner, 1, 0)
        row = 2 * owner + rank
        out[row, 0:ROWS, :] = total
        place = (homes[0, tile] - OWN * owner).astype(jnp.float32)
        out[row, ROWS:, :] = jnp.broadcast_to(place, (8, INNER))


def place_kernel(got, out, totals):
    for place in range(OWN):
        total = jnp.zeros((ROWS, INNER), jnp.float32)
        for source in range(2 * TM):
            hit = got[source, ROWS : ROWS + 1, :] == float(place)
            total = total + jnp.where(hit, got[source, 0:ROWS, :], 0.0)
        totals[place * ROWS : (place + 1) * ROWS, :] = total
    for row in range(ROWS):
        at = (row % 16) * INNER
        out[row // 16, :, at : at + INNER] = totals[pl.ds(row, OWN, stride=ROWS), :]


def call(kernel, outs, specs, *operands, scratch=()):
    operands = [
        pltpu.with_memory_space_constraint(o, HBM) if m is HBM else o
        for o, m in zip(operands, specs)
    ]
    return pl.pallas_call(
        kernel,
        out_shape=outs,
        in_specs=[pl.BlockSpec(memory_space=s) for s in specs],
        scratch_shapes=list(scratch),
        compiler_params=pltpu.CompilerParams(vmem_limit_bytes=48 << 20),
    )(*operands)


def per_device(
    timestream, polar_angle, pixel_index, strip_tile, time_const, knee_freq, noise_slope,
    white_weight, mode_mix, coupling, device_slots, slot_home,
):
    f32 = jnp.float32
    rows, forward, inverse = [jnp.asarray(t) for t in tables()]
    packed, weight = call(
        forward_kernel,
        (
            jax.ShapeDtypeStruct((PEERS, 48, INNER), f32),
            jax.ShapeDtypeStruct((PEERS, DETS, INNER), f32),
        ),
        [HBM] * 9,
        device_slots, timestream, time_const, knee_freq, noise_slope, white_weight,
        mode_mix, rows, forward,
        scratch=[
            VMEM((OUTER * DETS, 2 * INNER), f32),
            SMEM((1, PEERS), jnp.int32),
            VMEM((DETS, 2 * SAMPLES), f32),
            VMEM((1, DETS), f32),
            VMEM((1, DETS), f32),
            VMEM((1, DETS), f32),
            VMEM((1, DETS), f32),
            VMEM((DETS, MODES), f32),
            VMEM((4 * OUTER, INNER), f32),
            VMEM((2 * INNER, 2 * INNER), f32),
            SMEM((PEERS,), jnp.int32),
            pltpu.SemaphoreType.DMA((9,)),
        ],
    )
    got = lax.all_to_all(packed, "det", 0, 0, tiled=True)
    projected, labels = call(
        couple_kernel,
        (
            jax.ShapeDtypeStruct((PEERS, 2 * DETS, INNER), f32),
            jax.ShapeDtypeStruct((PEERS, 8, INNER), f32),
        ),
        [VMEM, HBM],
        got, coupling,
        scratch=[VMEM((MODES, MODES), f32), pltpu.SemaphoreType.DMA],
    )
    back = lax.all_to_all(projected, "det", 0, 0, tiled=True)
    twice = 2.0 * polar_angle[0]
    partials = call(
        bin_kernel,
        jax.ShapeDtypeStruct((2 * PEERS, ROWS, INNER), f32),
        [HBM] * 2 + [VMEM] * 5 + [HBM] * 3,
        device_slots, strip_tile, packed, weight, back, jnp.cos(twice), jnp.sin(twice),
        pixel_index, rows, inverse,
        scratch=[
            VMEM((OUTER * DETS, 2 * INNER), f32),
            VMEM((STRIPS, DETS, INNER), f32),
            SMEM((1, PEERS), jnp.int32),
            SMEM((DETS, STRIPS), jnp.int32),
            VMEM((DETS, 2 * SAMPLES), jnp.int32),
            VMEM((4 * OUTER, INNER), f32),
            VMEM((2, 2 * INNER, 2 * INNER), jnp.bfloat16),
            SMEM((PEERS,), jnp.int32),
            VMEM((UNROLL * 8 * DETS, INNER), f32),
            VMEM((PEERS, 2 * ROWS, INNER // 2), f32),
            VMEM((PEERS, 2 * ROWS, INNER // 2), f32),
            pltpu.SemaphoreType.DMA((5,)),
        ],
    )
    parts = lax.all_to_all(
        partials.reshape(PEERS, 2 * ROWS, INNER), "det", 0, 0, tiled=True
    )
    owned = call(
        gather_kernel,
        jax.ShapeDtypeStruct((2 * TM, ROWS + 8, INNER), f32),
        [SMEM] + [VMEM] * 2,
        slot_home, parts, labels,
    )
    final = lax.all_to_all(
        owned.reshape(TM, 2 * (ROWS + 8), INNER), "tm", 0, 0, tiled=True
    )
    placed = call(
        place_kernel,
        jax.ShapeDtypeStruct((3, OWN, 16 * INNER), f32),
        [VMEM],
        final.reshape(2 * TM, ROWS + 8, INNER),
        scratch=[VMEM((OWN * ROWS, INNER), f32)],
    )
    return placed.transpose(1, 0, 2)


def solution(mesh):
    strips = P("tm", "det", None)
    dets = P("tm", "det")
    return jax.shard_map(
        per_device,
        mesh=mesh,
        in_specs=(strips,) * 4 + (dets,) * 4 + (strips, P(), dets, dets),
        out_specs=P(("tm", "det"), None, None),
        check_vma=False,
    )
```

time: 138 us -> 100 us (0.72)
  Pallas kernels: 50.3 us -> 24.6 us
  local copies, waits for them, and re-layouts: 11.8 us -> 0.01 us
    pallas_call x5, Pallas kernels: 50.3 us -> 24.6 us  [call(): pl.pallas_call(kernel, out_shape=outs, in_specs=[pl.BlockSpec(memory_spac...]
    unnamed x40 -> x4, local copies, waits for them, and re-layouts: 10.9 us -> 0.01 us
where the time goes in v2:
time: 100 us
  blocking collectives  59.9 us (60%)
  Pallas kernels  24.6 us (25%)
  waiting for transfers between devices  9.7 us (10%)
  starting transfers between devices  3.9 us (4%)
  other arithmetic  1.88 us (2%)
    all_to_all x1, blocking collectives, per_device(): lax.all_to_all(partials.reshape(PEERS, 2 * ROWS, INNER), 'det', 0, 0, til...  26.3 us
    pallas_call x5, Pallas kernels, call(): pl.pallas_call(kernel, out_shape=outs, in_specs=[pl.BlockSpec(memory_spac...  24.6 us
    all_to_all x1, blocking collectives, per_device(): got = lax.all_to_all(packed, 'det', 0, 0, tiled=True)  22.9 us
    all_to_all x1, blocking collectives, per_device(): lax.all_to_all(owned.reshape(TM, 2 * (ROWS + 8), INNER), 'tm', 0, 0, tile...  10.7 us
    all_to_all x1, waiting for transfers between devices, per_device(): back = lax.all_to_all(projected, 'det', 0, 0, tiled=True)  9.7 us
    all_to_all x1, starting transfers between devices, per_device(): back = lax.all_to_all(projected, 'det', 0, 0, tiled=True)  3.9 us
  transfers between devices with their start and end apart: 1, of which 1 were waited for; matrix products, arithmetic and copies ran while one was open for 2% of the time, Pallas kernels for 0%

profile of v2, /device:TPU:0, one launch (start us, length us, event | category | flops | bytes accessed | tf_op | source)
XLA Modules:
  0.0 100.1 jit_solution(16613911665838845529)
XLA Ops:
  0.0 2.0 %shard_map.145 = (f32[32,48,128]{2,1,0:T(8,128)S(1)}, f32[32,16,128]{2,1,0:T(8,128)S(1)}) custom-call(s32[1,32]{1,0:T(1,128)} %slots_h.3, f32[1,16,8192]{2,1,0:T(8,128)} %signal_h.1, f32[1,16]{1,0:T(1,128)} %tau_h.1, f32[1,16]{1,0:T(1,128)} %knee_h.1, f32[1,16]{1,0:T(1,128)} %slope_h.1, f32[1,16]{1,0:T(1,128)} %white_h.1, f32[1,16,64]{2,1,0:T(8,128)} %mix_h.1, ...), custom_call_target="tpu_custom_call" | custom-call | tf_op jit(solution)/shard_map/pallas_call | solution.py:359
  2.0 0.0 copy-start.1
  2.0 22.9 %all_to_all.20.got = f32[32,48,128]{2,1,0:T(8,128)S(1)} all-to-all(f32[32,48,128]{2,1,0:T(8,128)S(1)} %get-tuple-element.9.weighted), channel_id=1, replica_groups=mesh['tm'=4,'det'=32] {'det'}, dimensions={0} | all-to-all | bytes 1572864 | tf_op jit(solution)/shard_map/all_to_all | solution.py:398
  24.9 2.2 %shard_map.146 = (f32[32,32,128]{2,1,0:T(8,128)}, f32[32,8,128]{2,1,0:T(8,128)S(1)}) custom-call(f32[32,48,128]{2,1,0:T(8,128)S(1)} %all_to_all.20.got, f32[64,64]{1,0:T(8,128)} %coupling_h.1), custom_call_target="tpu_custom_call" | custom-call | tf_op jit(solution)/shard_map/pallas_call | solution.py:359
  27.1 3.9 %all-to-all-start.1 = ((f32[32,32,128]{2,1,0:T(8,128)}), f32[32,32,128]{2,1,0:T(8,128)S(1)}, u32[]{:S(2)}, u32[]{:S(2)}) async-start(f32[32,32,128]{2,1,0:T(8,128)} %get-tuple-element.11), calls=%async_computation.1 | async-start | bytes 1048576 | tf_op jit(solution)/shard_map/all_to_all | solution.py:409
  31.0 0.0 copy-done.1
  31.1 1.9 %sine_bitcast_fusion = (f32[16,8192]{1,0:T(8,128)S(1)}, f32[16,8192]{1,0:T(8,128)S(1)}) fusion(f32[1,16,8192]{2,1,0:T(8,128)S(1)} %copy-done.1), kind=kLoop, calls=%fused_computation | loop fusion | flops 131072 | bytes 1572864 | tf_op jit(solution)/shard_map/sin | solution.py:415
  32.9 9.7 %all-to-all-done.1.back = f32[32,32,128]{2,1,0:T(8,128)S(1)} async-done(((f32[32,32,128]{2,1,0:T(8,128)}), f32[32,32,128]{2,1,0:T(8,128)S(1)}, u32[]{:S(2)}, u32[]{:S(2)}) %all-to-all-start.1) | async-done | bytes 524320 | tf_op jit(solution)/shard_map/all_to_all | solution.py:409
  42.6 18.3 %shard_map.147 = f32[64,48,128]{2,1,0:T(8,128)S(1)} custom-call(s32[1,32]{1,0:T(1,128)} %slots_h.3, s32[1,16,64]{2,1,0:T(8,128)} %tiles_h.1, f32[32,48,128]{2,1,0:T(8,128)S(1)} %get-tuple-element.9.weighted, f32[32,16,128]{2,1,0:T(8,128)S(1)} %get-tuple-element.10.weight, f32[32,32,128]{2,1,0:T(8,128)S(1)} %all-to-all-done.1.back, ...), custom_call_target="tpu_custom_call" | custom-call | tf_op jit(solution)/shard_map/pallas_call | solution.py:359
  60.9 0.0 copy-start
  60.9 26.3 %all_to_all.21.got = f32[32,96,128]{2,1,0:T(8,128)S(1)} all-to-all(f32[32,96,128]{2,1,0:T(8,128)S(1)} %bitcast.8), channel_id=1, replica_groups=mesh['tm'=4,'det'=32] {'det'}, dimensions={0} | all-to-all | bytes 3145728 | tf_op jit(solution)/shard_map/all_to_all | solution.py:432
  87.2 0.0 copy-done
  87.2 1.3 %shard_map.148 = f32[8,56,128]{2,1,0:T(8,128)S(1)} custom-call(s32[1,4]{1,0:T(1,128)S(1)} %copy-done, f32[32,96,128]{2,1,0:T(8,128)S(1)} %all_to_all.21.got, f32[32,8,128]{2,1,0:T(8,128)S(1)} %get-tuple-element.12.labels), custom_call_target="tpu_custom_call" | custom-call | tf_op jit(solution)/shard_map/pallas_call | solution.py:359
  88.5 10.7 %all_to_all.22 = f32[4,112,128]{2,1,0:T(8,128)S(1)} all-to-all(f32[4,112,128]{2,1,0:T(8,128)S(1)} %bitcast.10), channel_id=1, replica_groups=mesh['tm'=4,'det'=32] {'tm'}, dimensions={0} | all-to-all | bytes 458752 | tf_op jit(solution)/shard_map/all_to_all | solution.py:441
  99.2 0.9 shard_map.149
Async XLA Ops:
  2.0 29.0 %copy-start.1 = (f32[1,16,8192]{2,1,0:T(8,128)S(1)}, f32[1,16,8192]{2,1,0:T(8,128)}, u32[]{:S(2)}) copy-start(f32[1,16,8192]{2,1,0:T(8,128)} %param.16) | copy-start | bytes 1572868
  27.1 15.5 %all-to-all-start.1 = ((f32[32,32,128]{2,1,0:T(8,128)}), f32[32,32,128]{2,1,0:T(8,128)S(1)}, u32[]{:S(2)}, u32[]{:S(2)}) async-start(f32[32,32,128]{2,1,0:T(8,128)} %get-tuple-element.11), calls=%async_computation.1 | async-start | bytes 1048576 | tf_op jit(solution)/shard_map/all_to_all | solution.py:409
  60.9 26.3 %copy-start = (s32[1,4]{1,0:T(1,128)S(1)}, s32[1,4]{1,0:T(1,128)}, u32[]{:S(2)}) copy-start(s32[1,4]{1,0:T(1,128)} %homes.1) | copy-start | bytes 52

commit v3 on v2

--- a/solution.py
+++ b/solution.py
@@ -17,7 +17,8 @@
 MODES = 64
 TM = 4
 OWN = 8
-UNROLL = 4
+UNROLL = 8
+HOT = 8
 ROWS = 48
 
 HIGHEST = lax.Precision.HIGHEST
@@ -101,7 +102,7 @@
 
 def forward_kernel(
     slots_h, signal_h, tau_h, knee_h, slope_h, white_h, mix_h, rows_h, matrix_h,
-    out, weight_out, scratch, slots, signal, tau, knee, slope, white, mix, rows, matrix,
+    out, scratch, slots, signal, tau, knee, slope, white, mix, rows, matrix,
     counts, sems,
 ):
     pairs = [
@@ -140,11 +141,7 @@
             s = rows[OUTER + k : OUTER + k + 1, :]
             scratch[k * DETS + lo : k * DETS + lo + 8, 0:INNER] = re * c + im * s
             scratch[k * DETS + lo : k * DETS + lo + 8, INNER : 2 * INNER] = im * c - re * s
-    tau_c = jnp.broadcast_to(column(tau[...]), (DETS, INNER))
-    slope_c = jnp.broadcast_to(column(slope[...]), (DETS, INNER))
-    white_c = jnp.broadcast_to(column(white[...]), (DETS, INNER))
-    knee_c = jnp.broadcast_to(column(knee[...]), (DETS, INNER))
-    knee_p = jnp.exp(slope_c * jnp.log(knee_c))
+    tau_c, knee_p, slope_c, white_c = noise_params(tau, knee, slope, white)
     copies[8].wait()
     group = 8
     for start in range(0, OUTER, group):
@@ -161,7 +158,6 @@
             lag = tau_c * rows[3 * OUTER + k : 3 * OUTER + k + 1, :]
             re = spec[step * DETS : (step + 1) * DETS, 0:INNER]
             im = spec[step * DETS : (step + 1) * DETS, INNER : 2 * INNER]
-            weight_out[k] = weight
             out[k, 0:DETS, :] = weight * (re - lag * im)
             out[k, DETS : 2 * DETS, :] = weight * (im + lag * re)
 
@@ -192,10 +188,43 @@
     labels[...] = got[:, 40:48, :]
 
 
+def lane_marks():
+    lanes = lax.broadcasted_iota(jnp.int32, (INNER, INNER), 1).astype(jnp.float32)
+    return (
+        lanes.astype(jnp.bfloat16),
+        jnp.ones((INNER, INNER), jnp.bfloat16),
+        jnp.zeros((INNER, INNER), jnp.bfloat16),
+    )
+
+
+def noise_params(tau, knee, slope, white):
+    def wide(ref):
+        return jnp.broadcast_to(column(ref[...]), (DETS, INNER))
+
+    slope_c = wide(slope)
+    return wide(tau), jnp.exp(slope_c * jnp.log(wide(knee))), slope_c, wide(white)
+
+
+def hot_kernel(pixel, knee, slope, white, log_f, hot, lows, weight):
+    lanes, one, none = lane_marks()
+    pieces = [pixel[0, :, i * INNER : (i + 1) * INNER] & 127 for i in range(UNROLL)]
+    turned = jnp.concatenate(pieces, axis=0).astype(jnp.float32).T
+    lows[0] = turned
+    for step in range(UNROLL):
+        for d in range(0, DETS, HOT):
+            at = step * DETS + d
+            low_d = jnp.broadcast_to(turned[:, at : at + 1], (INNER, INNER))
+            hot[0, at // HOT] = jnp.where(low_d.astype(jnp.bfloat16) == lanes, one, none)
+    _, knee_p, slope_c, white_c = noise_params(knee, knee, slope, white)
+    for k in range(weight.shape[0]):
+        power = jnp.exp(slope_c * log_f[0, k : k + 1, :])
+        weight[k] = white_c * power / (power + knee_p)
+
+
 def bin_kernel(
     slots_h, tiles_h, weighted, weight, back, cosine, sine, pixel_h, rows_h, matrix_h,
-    out, scratch, stream, slots, tiles, pixel, rows, matrix, counts, parts,
-    even, odd, sems,
+    lows_h, hot_h, out, scratch, stream, slots, tiles, pixel, rows, matrix, counts, parts,
+    even, odd, hot, lows, sems, hot_sems, low_sems,
 ):
     pairs = [
         (matrix_h, matrix), (rows_h, rows), (slots_h, slots), (tiles_h.at[0], tiles),
@@ -203,6 +232,15 @@
     ]
     copies = [pltpu.make_async_copy(a, b, sems.at[i]) for i, (a, b) in enumerate(pairs)]
     for copy in copies:
+        copy.start()
+
+    def load(start, slot):
+        return (
+            pltpu.make_async_copy(hot_h.at[start], hot.at[slot], hot_sems.at[slot]),
+            pltpu.make_async_copy(lows_h.at[start], lows.at[slot], low_sems.at[slot]),
+        )
+
+    for copy in load(0, 0):
         copy.start()
     for k in range(OUTER):
         re = weighted[k, 0:DETS, :] - weight[k] * back[k, 0:DETS, :]
@@ -239,8 +277,8 @@
 
     def clear(entry, carry):
         blank = jnp.zeros((ROWS, INNER), jnp.float32)
-        even[entry] = jnp.zeros((2 * ROWS, INNER // 2), jnp.float32)
-        odd[entry] = jnp.zeros((2 * ROWS, INNER // 2), jnp.float32)
+        even[entry] = blank
+        odd[entry] = blank
         out[entry] = blank
         out[PEERS + entry] = blank
         return carry
@@ -248,12 +286,21 @@
     lax.fori_loop(0, PEERS, clear, 0)
     for copy in copies[2:]:
         copy.wait()
-    levels = lax.broadcasted_iota(jnp.int32, (16, INNER), 0).astype(jnp.float32)
-    marks = [(levels + 16.0 * g).astype(jnp.bfloat16) for g in range(8)]
-    one = jnp.ones((16, INNER), jnp.bfloat16)
+    levels = (lax.broadcasted_iota(jnp.int32, (16, INNER), 0) & 7).astype(jnp.float32)
+    marks = [(levels + 8.0 * g).astype(jnp.bfloat16) for g in range(2)]
     zero = jnp.zeros((16, INNER), jnp.bfloat16)
+    lanes, one, none = lane_marks()
 
     def block(start, carry):
+        slot = start & 1
+        for copy in load(start, slot):
+            copy.wait()
+
+        @pl.when(start + 1 < STRIPS // UNROLL)
+        def _():
+            for copy in load(start + 1, 1 - slot):
+                copy.start()
+
         for step in range(UNROLL):
             s = start * UNROLL + step
             base = pl.multiple_of(s * INNER, INNER)
@@ -266,49 +313,43 @@
             ]
             tops = [m.astype(jnp.bfloat16).astype(jnp.float32) for m in maps]
             rests = [m - t for m, t in zip(maps, tops)]
-            fields = [
-                ((pix >> 7) + 16 * ((pix >> 6) & 1)).astype(jnp.float32),
-                (pix & 63).astype(jnp.float32),
-            ]
-            for i, field in enumerate(fields + tops + rests):
-                at = (step * 8 + i) * DETS
+            for i, field in enumerate([(pix >> 7).astype(jnp.float32)] + tops + rests):
+                at = (step * 7 + i) * DETS
                 parts[at : at + DETS, :] = field
         for step in range(UNROLL):
             s = start * UNROLL + step
 
-            def spread(i, d):
-                row = (step * 8 + i) * DETS + d
-                wide = parts[pl.ds(row, 8, stride=0), :]
-                return jnp.concatenate([wide, wide], axis=0).astype(jnp.bfloat16)
+            def spread(i, j, d):
+                lines = [
+                    parts[pl.ds((step * 7 + n) * DETS + d, 8, stride=0), :] for n in (i, j)
+                ]
+                return jnp.concatenate(lines, axis=0).astype(jnp.bfloat16)
 
             for d in range(DETS):
-                low_d = spread(1, d)
-                high_d = spread(0, d)
-                hits = [high_d == marks[0], high_d == marks[1]]
+                at = step * DETS + d
+                high_d = spread(0, 0, d)
+                hits = [high_d == mark for mark in marks]
                 left = []
-                for c in range(6):
-                    value = spread(2 + c, d)
-                    left += [jnp.where(hit, value, zero) for hit in hits]
+                for c in range(3):
+                    both = spread(1 + c, 4 + c, d)
+                    left += [jnp.where(hit, both, zero) for hit in hits]
                 left = jnp.concatenate(left, axis=0)
-                right = jnp.concatenate(
-                    [jnp.where(low_d == marks[g], one, zero) for g in range(4)], axis=0
-                )
-                sums = lax.dot_general(
-                    left, right, (((1,), (1,)), ((), ())), preferred_element_type=jnp.float32
-                )
+                if d % HOT == 0:
+                    right = hot[slot, at // HOT]
+                else:
+                    low_d = jnp.broadcast_to(lows[slot, :, at : at + 1], (INNER, INNER))
+                    right = jnp.where(low_d.astype(jnp.bfloat16) == lanes, one, none)
+                sums = jnp.dot(left, right, preferred_element_type=jnp.float32)
                 tile = tiles[d, s]
                 total = (even, odd)[d % 2]
-                total[tile] = total[tile] + (sums[0 : 2 * ROWS, :] + sums[2 * ROWS :, :])
+                sums = sums.reshape(6, 2, 8, INNER)
+                total[tile] = total[tile] + (sums[:, 0] + sums[:, 1]).reshape(ROWS, INNER)
         return carry
 
     lax.fori_loop(0, STRIPS // UNROLL, block, 0)
 
     def settle(entry, slot, home, rank):
-        both = even[entry] + odd[entry]
-        for c in range(3):
-            out[2 * home + rank, 16 * c : 16 * c + 16, :] = jnp.concatenate(
-                [both[32 * c : 32 * c + 16, :], both[32 * c + 16 : 32 * c + 32, :]], axis=1
-            )
+        out[2 * home + rank] = even[entry] + odd[entry]
 
     ranks(slots, counts, settle)
 
@@ -361,7 +402,7 @@
         out_shape=outs,
         in_specs=[pl.BlockSpec(memory_space=s) for s in specs],
         scratch_shapes=list(scratch),
-        compiler_params=pltpu.CompilerParams(vmem_limit_bytes=48 << 20),
+        compiler_params=pltpu.CompilerParams(vmem_limit_bytes=9 << 20),
     )(*operands)
 
 
@@ -370,13 +411,11 @@
     white_weight, mode_mix, coupling, device_slots, slot_home,
 ):
     f32 = jnp.float32
-    rows, forward, inverse = [jnp.asarray(t) for t in tables()]
-    packed, weight = call(
+    table, forward, inverse = tables()
+    rows, forward, inverse = [jnp.asarray(t) for t in (table, forward, inverse)]
+    packed = call(
         forward_kernel,
-        (
-            jax.ShapeDtypeStruct((PEERS, 48, INNER), f32),
-            jax.ShapeDtypeStruct((PEERS, DETS, INNER), f32),
-        ),
+        jax.ShapeDtypeStruct((PEERS, 48, INNER), f32),
         [HBM] * 9,
         device_slots, timestream, time_const, knee_freq, noise_slope, white_weight,
         mode_mix, rows, forward,
@@ -407,13 +446,38 @@
         scratch=[VMEM((MODES, MODES), f32), pltpu.SemaphoreType.DMA],
     )
     back = lax.all_to_all(projected, "det", 0, 0, tiled=True)
+    blocks = STRIPS // UNROLL
+    width = UNROLL * INNER
+    halves = UNROLL * DETS // HOT
+    ks = OUTER // blocks
+    hot, lows, weight = pl.pallas_call(
+        hot_kernel,
+        out_shape=(
+            HBM((blocks, halves, INNER, INNER), jnp.bfloat16),
+            HBM((blocks, INNER, UNROLL * DETS), f32),
+            jax.ShapeDtypeStruct((OUTER, DETS, INNER), f32),
+        ),
+        grid=(blocks,),
+        in_specs=[pl.BlockSpec((1, DETS, width), lambda i: (0, 0, i))]
+        + [pl.BlockSpec((1, DETS), lambda i: (0, 0))] * 3
+        + [pl.BlockSpec((1, ks, INNER), lambda i: (i, 0, 0))],
+        out_specs=(
+            pl.BlockSpec((1, halves, INNER, INNER), lambda i: (i, 0, 0, 0)),
+            pl.BlockSpec((1, INNER, UNROLL * DETS), lambda i: (i, 0, 0)),
+            pl.BlockSpec((ks, DETS, INNER), lambda i: (i, 0, 0)),
+        ),
+        compiler_params=pltpu.CompilerParams(vmem_limit_bytes=9 << 20),
+    )(
+        pixel_index, knee_freq, noise_slope, white_weight,
+        jnp.asarray(table[2 * OUTER : 3 * OUTER].reshape(blocks, ks, INNER)),
+    )
     twice = 2.0 * polar_angle[0]
     partials = call(
         bin_kernel,
         jax.ShapeDtypeStruct((2 * PEERS, ROWS, INNER), f32),
-        [HBM] * 2 + [VMEM] * 5 + [HBM] * 3,
+        [HBM] * 2 + [VMEM] * 5 + [HBM] * 5,
         device_slots, strip_tile, packed, weight, back, jnp.cos(twice), jnp.sin(twice),
-        pixel_index, rows, inverse,
+        pixel_index, rows, inverse, lows, hot,
         scratch=[
             VMEM((OUTER * DETS, 2 * INNER), f32),
             VMEM((STRIPS, DETS, INNER), f32),
@@ -423,10 +487,14 @@
             VMEM((4 * OUTER, INNER), f32),
             VMEM((2, 2 * INNER, 2 * INNER), jnp.bfloat16),
             SMEM((PEERS,), jnp.int32),
-            VMEM((UNROLL * 8 * DETS, INNER), f32),
-            VMEM((PEERS, 2 * ROWS, INNER // 2), f32),
-            VMEM((PEERS, 2 * ROWS, INNER // 2), f32),
+            VMEM((UNROLL * 7 * DETS, INNER), f32),
+            VMEM((PEERS, ROWS, INNER), f32),
+            VMEM((PEERS, ROWS, INNER), f32),
+            VMEM((2, UNROLL * DETS // HOT, INNER, INNER), jnp.bfloat16),
+            VMEM((2, INNER, UNROLL * DETS), f32),
             pltpu.SemaphoreType.DMA((5,)),
+            pltpu.SemaphoreType.DMA((2,)),
+            pltpu.SemaphoreType.DMA((2,)),
         ],
     )
     parts = lax.all_to_all(

time: 100 us -> 95.9 us (0.959)
  waiting for transfers between devices: 9.7 us -> 3.51 us
    all_to_all x1, waiting for transfers between devices: 9.7 us -> 3.51 us  [per_device(): back = lax.all_to_all(projected, 'det', 0, 0, tiled=True)]
    pallas_call x0 -> x1, Pallas kernels: none -> 5.21 us  [per_device(): pl.pallas_call(hot_kernel, out_shape=(HBM((blocks, halves, INNER, INNER),...]
    pallas_call x5, Pallas kernels: 24.6 us -> 20 us  [call(): pl.pallas_call(kernel, out_shape=outs, in_specs=[pl.BlockSpec(memory_spac...]
  transfers between devices with their start and end apart: 1 -> 1, of which waited for: 1 -> 1; matrix products, arithmetic and copies ran while one was open for 2% -> 3% of each run, Pallas kernels for 0% -> 5%
where the time goes in v3:
time: 95.9 us; the launch traced here: 95.5 us
  blocking collectives  60 us (63%)
  Pallas kernels  25.2 us (26%)
  starting transfers between devices  3.9 us (4%)
  waiting for transfers between devices  3.51 us (4%)
  other arithmetic  2.81 us (3%)
    all_to_all x1, blocking collectives, per_device(): lax.all_to_all(partials.reshape(PEERS, 2 * ROWS, INNER), 'det', 0, 0, til...  26.5 us
    all_to_all x1, blocking collectives, per_device(): got = lax.all_to_all(packed, 'det', 0, 0, tiled=True)  22.8 us
    pallas_call x5, Pallas kernels, call(): pl.pallas_call(kernel, out_shape=outs, in_specs=[pl.BlockSpec(memory_spac...  20 us
    all_to_all x1, blocking collectives, per_device(): lax.all_to_all(owned.reshape(TM, 2 * (ROWS + 8), INNER), 'tm', 0, 0, tile...  10.7 us
    pallas_call x1, Pallas kernels, per_device(): pl.pallas_call(hot_kernel, out_shape=(HBM((blocks, halves, INNER, INNER),...  5.21 us
    all_to_all x1, starting transfers between devices, per_device(): back = lax.all_to_all(projected, 'det', 0, 0, tiled=True)  3.9 us
    all_to_all x1, waiting for transfers between devices, per_device(): back = lax.all_to_all(projected, 'det', 0, 0, tiled=True)  3.51 us
    sin x1, other arithmetic, per_device(): jnp.sin(twice)  2.81 us
  transfers between devices with their start and end apart: 1, of which 1 were waited for; matrix products, arithmetic and copies ran while one was open for 3% of the time, Pallas kernels for 5%

profile of v3, /device:TPU:0, one launch (start us, length us, event | category | flops | bytes accessed | tf_op | source)
XLA Modules:
  0.0 95.5 jit_solution(4781226975538758366)
XLA Ops:
  0.0 2.0 %shard_map.154.weighted = f32[32,48,128]{2,1,0:T(8,128)S(1)} custom-call(s32[1,32]{1,0:T(1,128)} %slots_h.3, f32[1,16,8192]{2,1,0:T(8,128)} %signal_h.1, f32[1,16]{1,0:T(1,128)} %tau_h.1, f32[1,16]{1,0:T(1,128)} %knee.1, f32[1,16]{1,0:T(1,128)} %slope.1, f32[1,16]{1,0:T(1,128)} %white.1, f32[1,16,64]{2,1,0:T(8,128)} %mix_h.1, ...), custom_call_target="tpu_custom_call" | custom-call | tf_op jit(solution)/shard_map/pallas_call | solution.py:400
  2.0 22.8 %all_to_all.20.got = f32[32,48,128]{2,1,0:T(8,128)S(1)} all-to-all(f32[32,48,128]{2,1,0:T(8,128)S(1)} %shard_map.154.weighted), channel_id=1, replica_groups=mesh['tm'=4,'det'=32] {'det'}, dimensions={0} | all-to-all | bytes 1572864 | tf_op jit(solution)/shard_map/all_to_all | solution.py:437
  24.8 0.0 copy-start
  24.8 0.0 copy-start.1
  24.8 0.0 copy-start.2
  24.8 0.0 copy-start.3
  24.8 0.0 copy-start.4
  24.8 2.2 %shard_map.156 = (f32[32,32,128]{2,1,0:T(8,128)}, f32[32,8,128]{2,1,0:T(8,128)S(1)}) custom-call(f32[32,48,128]{2,1,0:T(8,128)S(1)} %all_to_all.20.got, f32[64,64]{1,0:T(8,128)} %coupling_h.1), custom_call_target="tpu_custom_call" | custom-call | tf_op jit(solution)/shard_map/pallas_call | solution.py:400
  27.1 3.9 %all-to-all-start.1 = ((f32[32,32,128]{2,1,0:T(8,128)}), f32[32,32,128]{2,1,0:T(8,128)S(1)}, u32[]{:S(2)}, u32[]{:S(2)}) async-start(f32[32,32,128]{2,1,0:T(8,128)} %get-tuple-element.11), calls=%async_computation.1 | async-start | bytes 1048576 | tf_op jit(solution)/shard_map/all_to_all | solution.py:448
  31.0 2.8 %sine_bitcast_fusion = (f32[16,8192]{1,0:T(8,128)S(1)}, f32[16,8192]{1,0:T(8,128)S(1)}) fusion(f32[1,16,8192]{2,1,0:T(8,128)} %param.17), kind=kLoop, calls=%fused_computation | loop fusion | flops 131072 | bytes 1572864 | tf_op jit(solution)/shard_map/sin | solution.py:479
  33.8 0.0 copy-done
  33.8 0.0 copy-done.1
  33.8 0.0 copy-done.2
  33.8 0.0 copy-done.3
  33.8 0.0 copy-done.4
  33.8 5.2 %shard_map.155 = (bf16[8,16,128,128]{3,2,1,0:T(8,128)(2,1)}, f32[8,128,128]{2,1,0:T(8,128)}, f32[32,16,128]{2,1,0:T(8,128)S(1)}) custom-call(s32[1,16,8192]{2,1,0:T(8,128)S(1)} %copy-done, f32[1,16]{1,0:T(1,128)S(1)} %copy-done.2, f32[1,16]{1,0:T(1,128)S(1)} %copy-done.3, f32[1,16]{1,0:T(1,128)S(1)} %copy-done.4, f32[8,4,128]{2,1,0:T(4,128)S(1)} %copy-done.1), custom_call_target="tpu_custom_call" | custom-call | tf_op jit(solution)/shard_map/pallas_call | solution.py:453
  39.1 3.5 %all-to-all-done.1.back = f32[32,32,128]{2,1,0:T(8,128)S(1)} async-done(((f32[32,32,128]{2,1,0:T(8,128)}), f32[32,32,128]{2,1,0:T(8,128)S(1)}, u32[]{:S(2)}, u32[]{:S(2)}) %all-to-all-start.1) | async-done | bytes 524320 | tf_op jit(solution)/shard_map/all_to_all | solution.py:448
  42.6 13.6 %shard_map.157 = f32[64,48,128]{2,1,0:T(8,128)S(1)} custom-call(s32[1,32]{1,0:T(1,128)} %slots_h.3, s32[1,16,64]{2,1,0:T(8,128)} %tiles_h.1, f32[32,48,128]{2,1,0:T(8,128)S(1)} %shard_map.154.weighted, f32[32,16,128]{2,1,0:T(8,128)S(1)} %get-tuple-element.10.weight, f32[32,32,128]{2,1,0:T(8,128)S(1)} %all-to-all-done.1.back, ...), custom_call_target="tpu_custom_call" | custom-call | tf_op jit(solution)/shard_map/pallas_call | solution.py:400
  56.2 0.0 copy-start.5
  56.2 26.5 %all_to_all.21.got = f32[32,96,128]{2,1,0:T(8,128)S(1)} all-to-all(f32[32,96,128]{2,1,0:T(8,128)S(1)} %bitcast.8), channel_id=1, replica_groups=mesh['tm'=4,'det'=32] {'det'}, dimensions={0} | all-to-all | bytes 3145728 | tf_op jit(solution)/shard_map/all_to_all | solution.py:500
  82.7 0.0 copy-done.5
  82.7 1.3 %shard_map.158 = f32[8,56,128]{2,1,0:T(8,128)S(1)} custom-call(s32[1,4]{1,0:T(1,128)S(1)} %copy-done.5, f32[32,96,128]{2,1,0:T(8,128)S(1)} %all_to_all.21.got, f32[32,8,128]{2,1,0:T(8,128)S(1)} %get-tuple-element.14.labels), custom_call_target="tpu_custom_call" | custom-call | tf_op jit(solution)/shard_map/pallas_call | solution.py:400
  84.0 10.7 %all_to_all.22 = f32[4,112,128]{2,1,0:T(8,128)S(1)} all-to-all(f32[4,112,128]{2,1,0:T(8,128)S(1)} %bitcast.10), channel_id=1, replica_groups=mesh['tm'=4,'det'=32] {'tm'}, dimensions={0} | all-to-all | bytes 458752 | tf_op jit(solution)/shard_map/all_to_all | solution.py:509
  94.7 0.9 shard_map.159
Async XLA Ops:
  24.8 9.0 %copy-start = (s32[1,16,8192]{2,1,0:T(8,128)S(1)}, s32[1,16,8192]{2,1,0:T(8,128)}, u32[]{:S(2)}) copy-start(s32[1,16,8192]{2,1,0:T(8,128)} %pixel_h.1) | copy-start | bytes 1572868
  24.8 9.0 %copy-start.1 = (f32[8,4,128]{2,1,0:T(4,128)S(1)}, f32[8,4,128]{2,1,0:T(4,128)}, u32[]{:S(2)}) copy-start(f32[8,4,128]{2,1,0:T(4,128)} %constant.13.clone.log_f) | copy-start | bytes 49156
  24.8 9.0 %copy-start.2 = (f32[1,16]{1,0:T(1,128)S(1)}, f32[1,16]{1,0:T(1,128)}, u32[]{:S(2)}) copy-start(f32[1,16]{1,0:T(1,128)} %knee.1) | copy-start | bytes 196
  24.8 9.0 %copy-start.3 = (f32[1,16]{1,0:T(1,128)S(1)}, f32[1,16]{1,0:T(1,128)}, u32[]{:S(2)}) copy-start(f32[1,16]{1,0:T(1,128)} %slope.1) | copy-start | bytes 196
  24.8 9.0 %copy-start.4 = (f32[1,16]{1,0:T(1,128)S(1)}, f32[1,16]{1,0:T(1,128)}, u32[]{:S(2)}) copy-start(f32[1,16]{1,0:T(1,128)} %white.1) | copy-start | bytes 196
  27.1 15.5 %all-to-all-start.1 = ((f32[32,32,128]{2,1,0:T(8,128)}), f32[32,32,128]{2,1,0:T(8,128)S(1)}, u32[]{:S(2)}, u32[]{:S(2)}) async-start(f32[32,32,128]{2,1,0:T(8,128)} %get-tuple-element.11), calls=%async_computation.1 | async-start | bytes 1048576 | tf_op jit(solution)/shard_map/all_to_all | solution.py:448
  56.2 26.5 %copy-start.5 = (s32[1,4]{1,0:T(1,128)S(1)}, s32[1,4]{1,0:T(1,128)}, u32[]{:S(2)}) copy-start(s32[1,4]{1,0:T(1,128)} %homes.1) | copy-start | bytes 52

commit v4 on v3

--- a/solution.py
+++ b/solution.py
@@ -242,6 +242,15 @@
 
     for copy in load(0, 0):
         copy.start()
+    def clear(entry, carry):
+        blank = jnp.zeros((ROWS, INNER), jnp.float32)
+        even[entry] = blank
+        odd[entry] = blank
+        out[entry] = blank
+        out[PEERS + entry] = blank
+        return carry
+
+    lax.fori_loop(0, PEERS, clear, 0)
     for k in range(OUTER):
         re = weighted[k, 0:DETS, :] - weight[k] * back[k, 0:DETS, :]
         im = weighted[k, DETS : 2 * DETS, :] - weight[k] * back[k, DETS : 2 * DETS, :]
@@ -275,15 +284,6 @@
             stream[a, lo : lo + 8, :] = re
             stream[OUTER + a, lo : lo + 8, :] = im
 
-    def clear(entry, carry):
-        blank = jnp.zeros((ROWS, INNER), jnp.float32)
-        even[entry] = blank
-        odd[entry] = blank
-        out[entry] = blank
-        out[PEERS + entry] = blank
-        return carry
-
-    lax.fori_loop(0, PEERS, clear, 0)
     for copy in copies[2:]:
         copy.wait()
     levels = (lax.broadcasted_iota(jnp.int32, (16, INNER), 0) & 7).astype(jnp.float32)
@@ -358,18 +358,19 @@
     for place in range(2 * TM):
         out[place, 0:ROWS, :] = jnp.zeros((ROWS, INNER), jnp.float32)
         out[place, ROWS:, :] = jnp.full((8, INNER), -1.0, jnp.float32)
+    def add(source, totals):
+        totals = list(totals)
+        for rank in range(2):
+            slab = got[source, rank * ROWS : (rank + 1) * ROWS, :]
+            label = labels[source, rank : rank + 1, :]
+            for tile in range(4):
+                totals[tile] = totals[tile] + jnp.where(label == float(tile), slab, 0.0)
+        return tuple(totals)
+
+    blank = jnp.zeros((ROWS, INNER), jnp.float32)
+    totals = lax.fori_loop(0, PEERS, add, (blank,) * 4, unroll=4)
     for tile in range(4):
-        def add(source, total):
-            for rank in range(2):
-                hit = labels[source, rank : rank + 1, :] == float(tile)
-                total = total + jnp.where(
-                    hit, got[source, rank * ROWS : (rank + 1) * ROWS, :], 0.0
-                )
-            return total
-
-        total = lax.fori_loop(
-            0, PEERS, add, jnp.zeros((ROWS, INNER), jnp.float32), unroll=4
-        )
+        total = totals[tile]
         owner = homes[0, tile] // OWN
         rank = 0
         for other in range(tile):

time: 95.9 us -> 95.6 us (level)
  no operation moved by 1% of the time
where the time goes in v4:
time: 95.6 us; the launch traced here: 95.2 us
  blocking collectives  59.9 us (63%)
  Pallas kernels  24.9 us (26%)
  starting transfers between devices  3.9 us (4%)
  waiting for transfers between devices  3.51 us (4%)
  other arithmetic  2.81 us (3%)
    all_to_all x1, blocking collectives, per_device(): lax.all_to_all(partials.reshape(PEERS, 2 * ROWS, INNER), 'det', 0, 0, til...  26.5 us
    all_to_all x1, blocking collectives, per_device(): got = lax.all_to_all(packed, 'det', 0, 0, tiled=True)  22.8 us
    pallas_call x5, Pallas kernels, call(): pl.pallas_call(kernel, out_shape=outs, in_specs=[pl.BlockSpec(memory_spac...  19.7 us
    all_to_all x1, blocking collectives, per_device(): lax.all_to_all(owned.reshape(TM, 2 * (ROWS + 8), INNER), 'tm', 0, 0, tile...  10.7 us
    pallas_call x1, Pallas kernels, per_device(): pl.pallas_call(hot_kernel, out_shape=(HBM((blocks, halves, INNER, INNER),...  5.21 us
    all_to_all x1, starting transfers between devices, per_device(): back = lax.all_to_all(projected, 'det', 0, 0, tiled=True)  3.9 us
    all_to_all x1, waiting for transfers between devices, per_device(): back = lax.all_to_all(projected, 'det', 0, 0, tiled=True)  3.51 us
    sin x1, other arithmetic, per_device(): jnp.sin(twice)  2.81 us
  transfers between devices with their start and end apart: 1, of which 1 were waited for; matrix products, arithmetic and copies ran while one was open for 3% of the time, Pallas kernels for 5%

profile of v4, /device:TPU:0, one launch (start us, length us, event | category | flops | bytes accessed | tf_op | source)
XLA Modules:
  0.0 95.2 jit_solution(8261700537343096746)
XLA Ops:
  0.0 2.0 %shard_map.154.weighted = f32[32,48,128]{2,1,0:T(8,128)S(1)} custom-call(s32[1,32]{1,0:T(1,128)} %slots_h.3, f32[1,16,8192]{2,1,0:T(8,128)} %signal_h.1, f32[1,16]{1,0:T(1,128)} %tau_h.1, f32[1,16]{1,0:T(1,128)} %knee.1, f32[1,16]{1,0:T(1,128)} %slope.1, f32[1,16]{1,0:T(1,128)} %white.1, f32[1,16,64]{2,1,0:T(8,128)} %mix_h.1, ...), custom_call_target="tpu_custom_call" | custom-call | tf_op jit(solution)/shard_map/pallas_call | solution.py:401
  2.0 22.8 %all_to_all.20.got = f32[32,48,128]{2,1,0:T(8,128)S(1)} all-to-all(f32[32,48,128]{2,1,0:T(8,128)S(1)} %shard_map.154.weighted), channel_id=1, replica_groups=mesh['tm'=4,'det'=32] {'det'}, dimensions={0} | all-to-all | bytes 1572864 | tf_op jit(solution)/shard_map/all_to_all | solution.py:438
  24.8 0.0 copy-start
  24.8 0.0 copy-start.1
  24.8 0.0 copy-start.2
  24.8 0.0 copy-start.3
  24.8 0.0 copy-start.4
  24.8 2.2 %shard_map.156 = (f32[32,32,128]{2,1,0:T(8,128)}, f32[32,8,128]{2,1,0:T(8,128)S(1)}) custom-call(f32[32,48,128]{2,1,0:T(8,128)S(1)} %all_to_all.20.got, f32[64,64]{1,0:T(8,128)} %coupling_h.1), custom_call_target="tpu_custom_call" | custom-call | tf_op jit(solution)/shard_map/pallas_call | solution.py:401
  27.1 3.9 %all-to-all-start.1 = ((f32[32,32,128]{2,1,0:T(8,128)}), f32[32,32,128]{2,1,0:T(8,128)S(1)}, u32[]{:S(2)}, u32[]{:S(2)}) async-start(f32[32,32,128]{2,1,0:T(8,128)} %get-tuple-element.11), calls=%async_computation.1 | async-start | bytes 1048576 | tf_op jit(solution)/shard_map/all_to_all | solution.py:449
  31.0 2.8 %sine_bitcast_fusion = (f32[16,8192]{1,0:T(8,128)S(1)}, f32[16,8192]{1,0:T(8,128)S(1)}) fusion(f32[1,16,8192]{2,1,0:T(8,128)} %param.17), kind=kLoop, calls=%fused_computation | loop fusion | flops 131072 | bytes 1572864 | tf_op jit(solution)/shard_map/sin | solution.py:480
  33.8 0.0 copy-done
  33.8 0.0 copy-done.1
  33.8 0.0 copy-done.2
  33.8 0.0 copy-done.3
  33.8 0.0 copy-done.4
  33.8 5.2 %shard_map.155 = (bf16[8,16,128,128]{3,2,1,0:T(8,128)(2,1)}, f32[8,128,128]{2,1,0:T(8,128)}, f32[32,16,128]{2,1,0:T(8,128)S(1)}) custom-call(s32[1,16,8192]{2,1,0:T(8,128)S(1)} %copy-done, f32[1,16]{1,0:T(1,128)S(1)} %copy-done.2, f32[1,16]{1,0:T(1,128)S(1)} %copy-done.3, f32[1,16]{1,0:T(1,128)S(1)} %copy-done.4, f32[8,4,128]{2,1,0:T(4,128)S(1)} %copy-done.1), custom_call_target="tpu_custom_call" | custom-call | tf_op jit(solution)/shard_map/pallas_call | solution.py:454
  39.1 3.5 %all-to-all-done.1.back = f32[32,32,128]{2,1,0:T(8,128)S(1)} async-done(((f32[32,32,128]{2,1,0:T(8,128)}), f32[32,32,128]{2,1,0:T(8,128)S(1)}, u32[]{:S(2)}, u32[]{:S(2)}) %all-to-all-start.1) | async-done | bytes 524320 | tf_op jit(solution)/shard_map/all_to_all | solution.py:449
  42.6 13.3 %shard_map.157 = f32[64,48,128]{2,1,0:T(8,128)S(1)} custom-call(s32[1,32]{1,0:T(1,128)} %slots_h.3, s32[1,16,64]{2,1,0:T(8,128)} %tiles_h.1, f32[32,48,128]{2,1,0:T(8,128)S(1)} %shard_map.154.weighted, f32[32,16,128]{2,1,0:T(8,128)S(1)} %get-tuple-element.10.weight, f32[32,32,128]{2,1,0:T(8,128)S(1)} %all-to-all-done.1.back, ...), custom_call_target="tpu_custom_call" | custom-call | tf_op jit(solution)/shard_map/pallas_call | solution.py:401
  55.9 0.0 copy-start.5
  55.9 26.5 %all_to_all.21.got = f32[32,96,128]{2,1,0:T(8,128)S(1)} all-to-all(f32[32,96,128]{2,1,0:T(8,128)S(1)} %bitcast.8), channel_id=1, replica_groups=mesh['tm'=4,'det'=32] {'det'}, dimensions={0} | all-to-all | bytes 3145728 | tf_op jit(solution)/shard_map/all_to_all | solution.py:501
  82.4 0.0 copy-done.5
  82.4 1.2 %shard_map.158 = f32[8,56,128]{2,1,0:T(8,128)S(1)} custom-call(s32[1,4]{1,0:T(1,128)S(1)} %copy-done.5, f32[32,96,128]{2,1,0:T(8,128)S(1)} %all_to_all.21.got, f32[32,8,128]{2,1,0:T(8,128)S(1)} %get-tuple-element.14.labels), custom_call_target="tpu_custom_call" | custom-call | tf_op jit(solution)/shard_map/pallas_call | solution.py:401
  83.6 10.7 %all_to_all.22 = f32[4,112,128]{2,1,0:T(8,128)S(1)} all-to-all(f32[4,112,128]{2,1,0:T(8,128)S(1)} %bitcast.10), channel_id=1, replica_groups=mesh['tm'=4,'det'=32] {'tm'}, dimensions={0} | all-to-all | bytes 458752 | tf_op jit(solution)/shard_map/all_to_all | solution.py:510
  94.3 0.9 shard_map.159
Async XLA Ops:
  24.8 9.0 %copy-start = (s32[1,16,8192]{2,1,0:T(8,128)S(1)}, s32[1,16,8192]{2,1,0:T(8,128)}, u32[]{:S(2)}) copy-start(s32[1,16,8192]{2,1,0:T(8,128)} %pixel_h.1) | copy-start | bytes 1572868
  24.8 9.0 %copy-start.1 = (f32[8,4,128]{2,1,0:T(4,128)S(1)}, f32[8,4,128]{2,1,0:T(4,128)}, u32[]{:S(2)}) copy-start(f32[8,4,128]{2,1,0:T(4,128)} %constant.13.clone.log_f) | copy-start | bytes 49156
  24.8 9.0 %copy-start.2 = (f32[1,16]{1,0:T(1,128)S(1)}, f32[1,16]{1,0:T(1,128)}, u32[]{:S(2)}) copy-start(f32[1,16]{1,0:T(1,128)} %knee.1) | copy-start | bytes 196
  24.8 9.0 %copy-start.3 = (f32[1,16]{1,0:T(1,128)S(1)}, f32[1,16]{1,0:T(1,128)}, u32[]{:S(2)}) copy-start(f32[1,16]{1,0:T(1,128)} %slope.1) | copy-start | bytes 196
  24.8 9.0 %copy-start.4 = (f32[1,16]{1,0:T(1,128)S(1)}, f32[1,16]{1,0:T(1,128)}, u32[]{:S(2)}) copy-start(f32[1,16]{1,0:T(1,128)} %white.1) | copy-start | bytes 196
  27.1 15.5 %all-to-all-start.1 = ((f32[32,32,128]{2,1,0:T(8,128)}), f32[32,32,128]{2,1,0:T(8,128)S(1)}, u32[]{:S(2)}, u32[]{:S(2)}) async-start(f32[32,32,128]{2,1,0:T(8,128)} %get-tuple-element.11), calls=%async_computation.1 | async-start | bytes 1048576 | tf_op jit(solution)/shard_map/all_to_all | solution.py:449
  55.9 26.5 %copy-start.5 = (s32[1,4]{1,0:T(1,128)S(1)}, s32[1,4]{1,0:T(1,128)}, u32[]{:S(2)}) copy-start(s32[1,4]{1,0:T(1,128)} %homes.1) | copy-start | bytes 52

commit v5 on v4

--- a/solution.py
+++ b/solution.py
@@ -469,7 +469,7 @@
         ),
         compiler_params=pltpu.CompilerParams(vmem_limit_bytes=9 << 20),
     )(
-        pixel_index, knee_freq, noise_slope, white_weight,
+        pltpu.with_memory_space_constraint(pixel_index, HBM), knee_freq, noise_slope, white_weight,
         jnp.asarray(table[2 * OUTER : 3 * OUTER].reshape(blocks, ks, INNER)),
     )
     twice = 2.0 * polar_angle[0]

time: 95.6 us -> 96.7 us (1.012)
  Pallas kernels: 24.9 us -> 26.4 us
    pallas_call x1, Pallas kernels: 5.21 us -> 6.78 us  [per_device(): pl.pallas_call(hot_kernel, out_shape=(HBM((blocks, halves, INNER, INNER),...]
  transfers between devices with their start and end apart: 1 -> 1, of which waited for: 1 -> 1; matrix products, arithmetic and copies ran while one was open for 3% -> 2% of each run, Pallas kernels for 5% -> 7%
where the time goes in v5:
time: 96.7 us; the launch traced here: 95.9 us
  blocking collectives  60.7 us (63%)
  Pallas kernels  26.4 us (27%)
  starting transfers between devices  3.9 us (4%)
  waiting for transfers between devices  2.87 us (3%)
  other arithmetic  1.88 us (2%)
    all_to_all x1, blocking collectives, per_device(): lax.all_to_all(partials.reshape(PEERS, 2 * ROWS, INNER), 'det', 0, 0, til...  27.1 us
    all_to_all x1, blocking collectives, per_device(): got = lax.all_to_all(packed, 'det', 0, 0, tiled=True)  22.9 us
    pallas_call x5, Pallas kernels, call(): pl.pallas_call(kernel, out_shape=outs, in_specs=[pl.BlockSpec(memory_spac...  19.6 us
    all_to_all x1, blocking collectives, per_device(): lax.all_to_all(owned.reshape(TM, 2 * (ROWS + 8), INNER), 'tm', 0, 0, tile...  10.7 us
    pallas_call x1, Pallas kernels, per_device(): pl.pallas_call(hot_kernel, out_shape=(HBM((blocks, halves, INNER, INNER),...  6.78 us
    all_to_all x1, starting transfers between devices, per_device(): back = lax.all_to_all(projected, 'det', 0, 0, tiled=True)  3.9 us
    all_to_all x1, waiting for transfers between devices, per_device(): back = lax.all_to_all(projected, 'det', 0, 0, tiled=True)  2.87 us
  transfers between devices with their start and end apart: 1, of which 1 were waited for; matrix products, arithmetic and copies ran while one was open for 2% of the time, Pallas kernels for 7%

profile of v5, /device:TPU:0, one launch (start us, length us, event | category | flops | bytes accessed | tf_op | source)
XLA Modules:
  0.0 95.9 jit_solution(17532064166276364439)
XLA Ops:
  0.0 2.0 %shard_map.154.weighted = f32[32,48,128]{2,1,0:T(8,128)S(1)} custom-call(s32[1,32]{1,0:T(1,128)} %slots_h.3, f32[1,16,8192]{2,1,0:T(8,128)} %signal_h.1, f32[1,16]{1,0:T(1,128)} %tau_h.1, f32[1,16]{1,0:T(1,128)} %knee.1, f32[1,16]{1,0:T(1,128)} %slope.1, f32[1,16]{1,0:T(1,128)} %white.1, f32[1,16,64]{2,1,0:T(8,128)} %mix_h.1, ...), custom_call_target="tpu_custom_call" | custom-call | tf_op jit(solution)/shard_map/pallas_call | solution.py:401
  2.0 0.0 copy-start.5
  2.0 22.9 %all_to_all.20.got = f32[32,48,128]{2,1,0:T(8,128)S(1)} all-to-all(f32[32,48,128]{2,1,0:T(8,128)S(1)} %shard_map.154.weighted), channel_id=1, replica_groups=mesh['tm'=4,'det'=32] {'det'}, dimensions={0} | all-to-all | bytes 1572864 | tf_op jit(solution)/shard_map/all_to_all | solution.py:438
  24.9 0.0 copy-start
  24.9 0.0 copy-start.1
  24.9 0.0 copy-start.2
  24.9 0.0 copy-start.3
  25.0 2.2 %shard_map.156 = (f32[32,32,128]{2,1,0:T(8,128)}, f32[32,8,128]{2,1,0:T(8,128)S(1)}) custom-call(f32[32,48,128]{2,1,0:T(8,128)S(1)} %all_to_all.20.got, f32[64,64]{1,0:T(8,128)} %coupling_h.1), custom_call_target="tpu_custom_call" | custom-call | tf_op jit(solution)/shard_map/pallas_call | solution.py:401
  27.2 3.9 %all-to-all-start.1 = ((f32[32,32,128]{2,1,0:T(8,128)}), f32[32,32,128]{2,1,0:T(8,128)S(1)}, u32[]{:S(2)}, u32[]{:S(2)}) async-start(f32[32,32,128]{2,1,0:T(8,128)} %get-tuple-element.11), calls=%async_computation.1 | async-start | bytes 1048576 | tf_op jit(solution)/shard_map/all_to_all | solution.py:449
  31.1 0.0 copy-done.5
  31.1 1.9 %sine_bitcast_fusion = (f32[16,8192]{1,0:T(8,128)S(1)}, f32[16,8192]{1,0:T(8,128)S(1)}) fusion(f32[1,16,8192]{2,1,0:T(8,128)S(1)} %copy-done.5), kind=kLoop, calls=%fused_computation | loop fusion | flops 131072 | bytes 1572864 | tf_op jit(solution)/shard_map/sin | solution.py:480
  33.0 0.0 copy-done
  33.0 0.0 copy-done.1
  33.0 0.0 copy-done.2
  33.0 0.0 copy-done.3
  33.0 6.8 %shard_map.155 = (bf16[8,16,128,128]{3,2,1,0:T(8,128)(2,1)}, f32[8,128,128]{2,1,0:T(8,128)}, f32[32,16,128]{2,1,0:T(8,128)S(1)}) custom-call(s32[1,16,8192]{2,1,0:T(8,128)} %pixel_h.1, f32[1,16]{1,0:T(1,128)S(1)} %copy-done.1, f32[1,16]{1,0:T(1,128)S(1)} %copy-done.2, f32[1,16]{1,0:T(1,128)S(1)} %copy-done.3, f32[8,4,128]{2,1,0:T(4,128)S(1)} %copy-done), custom_call_target="tpu_custom_call" | custom-call | tf_op jit(solution)/shard_map/pallas_call | solution.py:454
  39.8 2.9 %all-to-all-done.1.back = f32[32,32,128]{2,1,0:T(8,128)S(1)} async-done(((f32[32,32,128]{2,1,0:T(8,128)}), f32[32,32,128]{2,1,0:T(8,128)S(1)}, u32[]{:S(2)}, u32[]{:S(2)}) %all-to-all-start.1) | async-done | bytes 524320 | tf_op jit(solution)/shard_map/all_to_all | solution.py:449
  42.7 13.3 %shard_map.157 = f32[64,48,128]{2,1,0:T(8,128)S(1)} custom-call(s32[1,32]{1,0:T(1,128)} %slots_h.3, s32[1,16,64]{2,1,0:T(8,128)} %tiles_h.1, f32[32,48,128]{2,1,0:T(8,128)S(1)} %shard_map.154.weighted, f32[32,16,128]{2,1,0:T(8,128)S(1)} %get-tuple-element.10.weight, f32[32,32,128]{2,1,0:T(8,128)S(1)} %all-to-all-done.1.back, ...), custom_call_target="tpu_custom_call" | custom-call | tf_op jit(solution)/shard_map/pallas_call | solution.py:401
  56.0 0.0 copy-start.4
  56.0 27.1 %all_to_all.21.got = f32[32,96,128]{2,1,0:T(8,128)S(1)} all-to-all(f32[32,96,128]{2,1,0:T(8,128)S(1)} %bitcast.8), channel_id=1, replica_groups=mesh['tm'=4,'det'=32] {'det'}, dimensions={0} | all-to-all | bytes 3145728 | tf_op jit(solution)/shard_map/all_to_all | solution.py:501
  83.2 0.0 copy-done.4
  83.2 1.2 %shard_map.158 = f32[8,56,128]{2,1,0:T(8,128)S(1)} custom-call(s32[1,4]{1,0:T(1,128)S(1)} %copy-done.4, f32[32,96,128]{2,1,0:T(8,128)S(1)} %all_to_all.21.got, f32[32,8,128]{2,1,0:T(8,128)S(1)} %get-tuple-element.14.labels), custom_call_target="tpu_custom_call" | custom-call | tf_op jit(solution)/shard_map/pallas_call | solution.py:401
  84.4 10.7 %all_to_all.22 = f32[4,112,128]{2,1,0:T(8,128)S(1)} all-to-all(f32[4,112,128]{2,1,0:T(8,128)S(1)} %bitcast.10), channel_id=1, replica_groups=mesh['tm'=4,'det'=32] {'tm'}, dimensions={0} | all-to-all | bytes 458752 | tf_op jit(solution)/shard_map/all_to_all | solution.py:510
  95.1 0.9 shard_map.159
Async XLA Ops:
  2.0 29.0 %copy-start.5 = (f32[1,16,8192]{2,1,0:T(8,128)S(1)}, f32[1,16,8192]{2,1,0:T(8,128)}, u32[]{:S(2)}) copy-start(f32[1,16,8192]{2,1,0:T(8,128)} %param.17) | copy-start | bytes 1572868
  24.9 8.0 %copy-start = (f32[8,4,128]{2,1,0:T(4,128)S(1)}, f32[8,4,128]{2,1,0:T(4,128)}, u32[]{:S(2)}) copy-start(f32[8,4,128]{2,1,0:T(4,128)} %constant.13.clone.log_f) | copy-start | bytes 49156
  24.9 8.0 %copy-start.1 = (f32[1,16]{1,0:T(1,128)S(1)}, f32[1,16]{1,0:T(1,128)}, u32[]{:S(2)}) copy-start(f32[1,16]{1,0:T(1,128)} %knee.1) | copy-start | bytes 196
  24.9 8.0 %copy-start.2 = (f32[1,16]{1,0:T(1,128)S(1)}, f32[1,16]{1,0:T(1,128)}, u32[]{:S(2)}) copy-start(f32[1,16]{1,0:T(1,128)} %slope.1) | copy-start | bytes 196
  24.9 8.1 %copy-start.3 = (f32[1,16]{1,0:T(1,128)S(1)}, f32[1,16]{1,0:T(1,128)}, u32[]{:S(2)}) copy-start(f32[1,16]{1,0:T(1,128)} %white.1) | copy-start | bytes 196
  27.2 15.5 %all-to-all-start.1 = ((f32[32,32,128]{2,1,0:T(8,128)}), f32[32,32,128]{2,1,0:T(8,128)S(1)}, u32[]{:S(2)}, u32[]{:S(2)}) async-start(f32[32,32,128]{2,1,0:T(8,128)} %get-tuple-element.11), calls=%async_computation.1 | async-start | bytes 1048576 | tf_op jit(solution)/shard_map/all_to_all | solution.py:449
  56.0 27.2 %copy-start.4 = (s32[1,4]{1,0:T(1,128)S(1)}, s32[1,4]{1,0:T(1,128)}, u32[]{:S(2)}) copy-start(s32[1,4]{1,0:T(1,128)} %homes.1) | copy-start | bytes 52
